TPU v7x, 32 devices: a whole 2x2x4 slice. The times are simulated.
32 devices in a mesh: groups: 2 (over y), ctx: 4 (over z), exp: 2 (over x), tp: 2 (over core).
Axes of the slice: x: 2, y: 2, z: 4, core: 2. Of those that a mesh axis runs over, the one named last changes fastest.
Arguments:
- queries: bfloat16 [4, 512, 20, 128], P(('groups', 'exp'), 'ctx', 'tp'), parts along dimension 0, may hold values from -9 to 9
- key_states: bfloat16 [4, 512, 4, 128], P(('groups', 'exp'), 'ctx', 'tp'), parts along dimension 0, may hold values from -9 to 9
- values: bfloat16 [4, 512, 4, 128], P(('groups', 'exp'), 'ctx', 'tp'), parts along dimension 0, may hold values from -6 to 6
- doc_ids: int32 [4, 512], P(('groups', 'exp'), 'ctx'), parts along dimension 0, may hold values from 0 to 3, never falling along the last dimension, each value on 1 to 256 neighbouring positions
- residual: bfloat16 [4, 512, 5120], P(('groups', 'exp'), ('ctx', 'tp')), parts along dimension 0, may hold values from -6 to 6
- out_proj: bfloat16 [2560, 5120], P('tp', 'ctx'), may hold values from -0.125 to 0.125
- norm_gain: bfloat16 [5120], replicated, may hold values from 0.5 to 1.5
- router: bfloat16 [5120, 64], P(None, 'exp'), may hold values from -0.078125 to 0.078125
- expert_ids: int32 [4, 512, 1], P(('groups', 'exp'), ('ctx', 'tp')), parts along dimension 0, may hold values from 0 to 63; in each aligned block of 64 rows (0 to 63, 64 to 127, ..., all dimensions but the last counted through in order) at most 2 rows name the same one
- keep_counts: int32 [128], P('groups'), parts along dimension 0, may hold values from 1 to 2
Outputs:
- expert_inputs: bfloat16 [32, 64, 2, 5120], P(('groups', 'ctx', 'tp'), 'exp'), parts along dimension 0
There are 2 independent parts, one for each index of `groups`. A program takes and returns all parts, laid end to end along the dimension named above; an argument that names none is the same for every part. Nothing has to cross between parts.
Inputs may be any that keep to these rules, and one draw needn't show every extreme that they name: `doc_ids`: doc ids never fall along a request; a document holds at most 256 tokens, and some document holds exactly that many. `expert_ids`: in each aligned block of 64 tokens (the rows of one device) no expert is named more than 2 times, and in some blocks one expert is named exactly 2 times.
All inputs are finite; a program needn't handle non-finite values.
Results may differ from a plain program's by a relative error of at most 0.013.
Values may be sent and summed in bfloat16 or wider, within the bound.
A program may use at most 64 MiB of HBM per device.

v0:
```python
import functools
import math

import jax
import jax.numpy as jnp
from jax import lax
from jax.experimental import pallas as pl
from jax.experimental.pallas import tpu as pltpu
from jax.sharding import PartitionSpec as P

CAP = 2
EPSILON = 1e-05
MESH = pl.DeviceIdType.MESH


def kernel(
    sizes,
    q_ref,
    key_ref,
    value_ref,
    doc_ref,
    residual_hbm,
    weight_hbm,
    gain_ref,
    router_ref,
    ids_ref,
    keep_ref,
    out_ref,
    kv_out,
    kv_in,
    gain,
    tally,
    doc_in,
    attn,
    weight,
    residual,
    product,
    part_out,
    part_in,
    res_out,
    res_in,
    slot_out,
    slot_in,
    load_sem,
    kv_send,
    kv_recv,
    doc_send,
    doc_recv,
    right_send,
    left_send,
    attn_recv,
    part_send,
    part_recv,
    res_send,
    res_recv,
    slot_send,
    slot_recv,
):
    ctx_count, exp_count, back, pieces = sizes
    heads, tokens, size = q_ref.shape
    groups = kv_out.shape[0]
    ratio = heads // groups
    half = tokens // 2
    columns = weight.shape[1]
    depth = weight.shape[0] // groups
    slots = slot_in.shape[3]
    part = columns // pieces
    me = lax.axis_index("ctx")
    mine = lax.axis_index("exp")
    core = lax.axis_index("tp")

    load_weight = pltpu.make_async_copy(weight_hbm, weight, load_sem.at[0])
    load_weight.start()
    aligned = columns % 128 == 0
    load_residual = []
    for block in range(ctx_count):
        there = slice(block * columns, (block + 1) * columns)
        load_residual.append(
            pltpu.make_async_copy(
                residual_hbm.at[:, there] if aligned else residual_hbm.at[block],
                residual.at[block],
                load_sem.at[1 + block],
            )
        )
        load_residual[-1].start()

    barrier = pltpu.get_barrier_semaphore()
    for shift in range(1, ctx_count):
        pl.semaphore_signal(
            barrier,
            inc=1,
            device_id={"ctx": lax.rem(me + shift, ctx_count)},
            device_id_type=MESH,
        )
    for shift in range(1, exp_count):
        pl.semaphore_signal(
            barrier,
            inc=1,
            device_id={"exp": lax.rem(mine + shift, exp_count)},
            device_id_type=MESH,
        )
    pl.semaphore_signal(barrier, inc=1, device_id={"tp": 1 - core}, device_id_type=MESH)

    for group in range(groups):
        kv_out[group, 0] = key_ref[:, group, :]
        kv_out[group, 1] = value_ref[:, group, :]

    pl.semaphore_wait(barrier, ctx_count + exp_count - 1)

    def kv_copy(group, shift):
        return pltpu.make_async_remote_copy(
            src_ref=kv_out.at[group],
            dst_ref=kv_in.at[group, shift - 1],
            send_sem=kv_send.at[group, shift - 1],
            recv_sem=kv_recv.at[group, shift - 1],
            device_id={"ctx": lax.rem(me + shift, ctx_count)},
            device_id_type=MESH,
        )

    def doc_copy(shift):
        return pltpu.make_async_remote_copy(
            src_ref=doc_ref,
            dst_ref=doc_in.at[shift - 1],
            send_sem=doc_send.at[shift - 1],
            recv_sem=doc_recv.at[shift - 1],
            device_id={"ctx": lax.rem(me + shift, ctx_count)},
            device_id_type=MESH,
        )

    for shift in range(1, back + 1):

        @pl.when(me + shift < ctx_count)
        def _(shift=shift):
            doc_copy(shift).start()

    for group in range(groups):
        for shift in range(1, back + 1):

            @pl.when(me + shift < ctx_count)
            def _(group=group, shift=shift):
                kv_copy(group, shift).start()

    row = lax.broadcasted_iota(jnp.int32, (half, half), 0)
    lane = lax.broadcasted_iota(jnp.int32, (half, half), 1)
    ids_row = ids_ref[...]
    ids_column = jnp.sum(jnp.where(row == lane, ids_row, 0), axis=1, keepdims=True)
    ranking = jnp.sum(
        jnp.where((ids_column == ids_row) & (row < lane), 1, 0), axis=0, keepdims=True
    )
    experts = keep_ref.shape[1]
    square_row = lax.broadcasted_iota(jnp.int32, (experts, experts), 0)
    square_lane = lax.broadcasted_iota(jnp.int32, (experts, experts), 1)
    keep_column = jnp.sum(
        jnp.where(square_row == square_lane, keep_ref[...], 0), axis=1, keepdims=True
    )
    expert_row = lax.broadcasted_iota(jnp.int32, (experts, half), 0)
    limits = jnp.sum(jnp.where(expert_row == ids_row, keep_column, 0), axis=0, keepdims=True)
    target = jnp.where(ranking < limits, ids_row * CAP + ranking, -1)
    slot_row = lax.broadcasted_iota(jnp.int32, (slots, half), 0)

    wide = gain_ref[...].astype(jnp.float32)
    for line in range(wide.shape[0]):
        gain[:, line * 128 : (line + 1) * 128] = wide[line : line + 1]

    for shift in range(1, back + 1):

        @pl.when(me < shift)
        def _(shift=shift):
            doc_in[shift - 1] = jnp.full(doc_in.shape[1:], -1, jnp.int32)
            for group in range(groups):
                kv_in[group, shift - 1] = jnp.zeros(kv_in.shape[2:], kv_in.dtype)

        @pl.when(me >= shift)
        def _(shift=shift):
            doc_copy(shift).wait_recv()

    square = lax.broadcasted_iota(jnp.int32, (tokens, tokens), 0)
    across = lax.broadcasted_iota(jnp.int32, (tokens, tokens), 1)
    doc_row = doc_ref[...]
    doc_column = jnp.sum(jnp.where(square == across, doc_row, 0), axis=1, keepdims=True)
    allowed = [(across <= square) & (doc_row == doc_column)]
    for shift in range(1, back + 1):
        allowed.append(doc_in[shift - 1] == doc_column)
    allowed = jnp.concatenate(
        [jnp.where(piece, 1.0, 0.0) for piece in allowed], axis=1
    )
    allowed = allowed > 0.5
    scale = 1.0 / math.sqrt(size)

    def attn_copy(block, group, rightward):
        to = me + 1 if rightward else me - 1
        sends = right_send if rightward else left_send
        return pltpu.make_async_remote_copy(
            src_ref=attn.at[block, group],
            dst_ref=attn.at[block, group],
            send_sem=sends.at[block, group],
            recv_sem=attn_recv.at[block, group],
            device_id={"ctx": lax.rem(to + ctx_count, ctx_count)},
            device_id_type=MESH,
        )

    for group in range(groups):
        for shift in range(1, back + 1):

            @pl.when(me >= shift)
            def _(group=group, shift=shift):
                kv_copy(group, shift).wait_recv()

        keys = jnp.concatenate(
            [kv_out[group, 0]] + [kv_in[group, shift, 0] for shift in range(back)], axis=0
        )
        vals = jnp.concatenate(
            [kv_out[group, 1]] + [kv_in[group, shift, 1] for shift in range(back)], axis=0
        )
        for head in range(ratio):
            scores = (
                lax.dot_general(
                    q_ref[group * ratio + head],
                    keys,
                    (((1,), (1,)), ((), ())),
                    preferred_element_type=jnp.float32,
                )
                * scale
            )
            masked = jnp.where(allowed, scores, -1e30)
            highest = jnp.max(masked, axis=1, keepdims=True)
            weights = jnp.where(allowed, jnp.exp(masked - highest), 0.0)
            totals = jnp.sum(weights, axis=1, keepdims=True)
            mixed = jnp.dot(weights.astype(jnp.bfloat16), vals, preferred_element_type=jnp.float32)
            attn[me, group, :, head * size : (head + 1) * size] = (mixed / totals).astype(
                jnp.bfloat16
            )

        @pl.when(me < ctx_count - 1)
        def _(group=group):
            attn_copy(me, group, True).start()

        @pl.when(me > 0)
        def _(group=group):
            attn_copy(me, group, False).start()

    def part_copy(block, piece):
        return pltpu.make_async_remote_copy(
            src_ref=part_out.at[block, piece],
            dst_ref=part_in.at[block, piece],
            send_sem=part_send.at[block, piece],
            recv_sem=part_recv.at[block, piece],
            device_id={"tp": 1 - core},
            device_id_type=MESH,
        )

    def res_copy(block, peer, piece):
        return pltpu.make_async_remote_copy(
            src_ref=res_out.at[block, piece],
            dst_ref=res_in.at[me, piece],
            send_sem=res_send.at[block, piece],
            recv_sem=res_recv.at[peer, piece],
            device_id={"ctx": block},
            device_id_type=MESH,
        )

    def slot_copy(shift, block, peer, piece):
        return pltpu.make_async_remote_copy(
            src_ref=slot_out.at[shift - 1, block, piece],
            dst_ref=slot_in.at[mine, block, piece],
            send_sem=slot_send.at[shift - 1, block, piece],
            recv_sem=slot_recv.at[peer, block, piece],
            device_id={"exp": lax.rem(mine + shift, exp_count)},
            device_id_type=MESH,
        )

    tile = math.gcd(part, 640)

    def project(block, piece):
        for first in range(0, part, tile):
            there = slice(piece * part + first, piece * part + first + tile)
            total = None
            for group in range(groups):
                term = jnp.dot(
                    attn[block, group],
                    weight[group * depth : (group + 1) * depth, there],
                    preferred_element_type=jnp.float32,
                )
                total = term if total is None else total + term
            product[block, piece, 0, :, first : first + tile] = total[:half]
            product[block, piece, 1, :, first : first + tile] = total[half:]
        part_out[block, piece] = product[block, piece, 1 - core].astype(jnp.bfloat16)
        part_copy(block, piece).start()

    def finish(block, piece):
        part_copy(block, piece).wait_recv()
        return (
            product[block, piece, core] + part_in[block, piece].astype(jnp.float32)
        ).astype(jnp.bfloat16)

    def place(block, piece):
        hidden = (
            residual[block, :, piece * part : (piece + 1) * part].astype(jnp.float32)
            + res_in[block, piece].astype(jnp.float32)
        ).astype(jnp.bfloat16)
        for shift in (*range(1, exp_count), 0):
            peer = lax.rem(mine + shift, exp_count)
            table = (slot_row + peer * slots == target).astype(jnp.bfloat16)
            chosen = jnp.dot(table, hidden, preferred_element_type=jnp.float32).astype(
                jnp.bfloat16
            )
            if shift == 0:
                slot_in[mine, block, piece] = chosen
            else:
                slot_out[shift - 1, block, piece] = chosen
                slot_copy(shift, block, mine, piece).start()

    load_weight.wait()
    for piece in range(pieces):
        project(me, piece)
    for load in load_residual:
        load.wait()
    for piece in range(pieces):
        res_in[me, piece] = finish(me, piece)
        place(me, piece)

    def step(distance, carry):
        left, right = me - distance, me + distance
        inside = distance < ctx_count
        has_left = (left >= 0) & inside
        has_right = (right < ctx_count) & inside

        @pl.when(has_left)
        def _():
            for group in range(groups):
                attn_copy(left, group, True).wait_recv()

                @pl.when(me < ctx_count - 1)
                def _():
                    attn_copy(left, group, True).start()

        @pl.when(has_right)
        def _():
            for group in range(groups):
                attn_copy(right, group, False).wait_recv()

                @pl.when(me > 0)
                def _():
                    attn_copy(right, group, False).start()

        for piece in range(pieces):
            for block, has in ((left, has_left), (right, has_right)):

                @pl.when(has)
                def _(block=block):
                    project(block, piece)

        for piece in range(pieces):
            for block, has in ((left, has_left), (right, has_right)):

                @pl.when(has)
                def _(block=block):
                    res_out[block, piece] = finish(block, piece)
                    res_copy(block, me, piece).start()

        for piece in range(pieces):
            for block, ok in (
                (left + 1, (left + 1 >= 0) & (distance >= 2)),
                (right - 1, (right - 1 < ctx_count) & (distance >= 2)),
            ):

                @pl.when(ok)
                def _(block=block):
                    res_copy(me, block, piece).wait_recv()
                    place(block, piece)

        return carry

    lax.fori_loop(1, ctx_count + 1, step, 0)

    spread = lax.broadcasted_iota(jnp.int32, (slots, router_ref.shape[0]), 0) // CAP
    expert = lax.broadcasted_iota(jnp.int32, (slots, router_ref.shape[0]), 1)
    for shift in range(exp_count):
        peer = lax.rem(mine + shift, exp_count)
        tally[...] = jnp.zeros_like(tally)

        def absorb(block):
            for piece in range(pieces):
                if shift:
                    slot_copy(1, block, peer, piece).wait_recv()
                hidden = slot_in[peer, block, piece].astype(jnp.float32)
                tally[:, :1] += jnp.sum(hidden * hidden, axis=1, keepdims=True)

        absorb(me)

        def gather(distance, carry):
            @pl.when(me >= distance)
            def _():
                absorb(me - distance)

            @pl.when(me + distance < ctx_count)
            def _():
                absorb(me + distance)

            return carry

        lax.fori_loop(1, ctx_count, gather, 0)
        factor = lax.rsqrt(tally[:, :1] / (columns * ctx_count) + EPSILON)
        logits = 0.0
        for block in range(ctx_count):
            for piece in range(pieces):
                first = block * columns + piece * part
                there = slice(first, first + part)
                normed = (
                    slot_in[peer, block, piece].astype(jnp.float32) * factor * gain[:, there]
                ).astype(jnp.bfloat16)
                slot_in[peer, block, piece] = normed
                logits = logits + lax.dot_general(
                    normed,
                    router_ref[:, there],
                    (((1,), (1,)), ((), ())),
                    preferred_element_type=jnp.float32,
                )
        logit = jnp.sum(jnp.where(spread == expert, logits, 0.0), axis=1, keepdims=True)
        gate = jax.nn.sigmoid(logit)
        for block in range(ctx_count):
            for piece in range(pieces):
                first = block * columns + piece * part
                done = slot_in[peer, block, piece].astype(jnp.float32) * gate
                out_ref[peer, :, :, first : first + part] = done.reshape(
                    slots // CAP, CAP, part
                ).astype(jnp.bfloat16)

    for shift in range(1, back + 1):

        @pl.when(me + shift < ctx_count)
        def _(shift=shift):
            doc_copy(shift).wait_send()
            for group in range(groups):
                kv_copy(group, shift).wait_send()

    def drain(block, carry):
        for piece in range(pieces):
            part_copy(block, piece).wait_send()
            for shift in range(1, exp_count):
                slot_copy(shift, block, mine, piece).wait_send()

        @pl.when(block != me)
        def _():
            for piece in range(pieces):
                res_copy(block, me, piece).wait_send()

        for group in range(groups):

            @pl.when((block <= me) & (me < ctx_count - 1))
            def _(group=group):
                attn_copy(block, group, True).wait_send()

            @pl.when((block >= me) & (me > 0))
            def _(group=group):
                attn_copy(block, group, False).wait_send()

        return carry

    lax.fori_loop(0, ctx_count, drain, 0)


def on_device(
    queries,
    key_states,
    values,
    doc_ids,
    residual,
    out_proj,
    norm_gain,
    router,
    expert_ids,
    keep_counts,
):
    tokens, heads, size = queries.shape[1:]
    groups = key_states.shape[2]
    ctx_count = lax.axis_size("ctx")
    exp_count = lax.axis_size("exp")
    features, columns = out_proj.shape
    half = residual.shape[1]
    width = residual.shape[2]
    experts = keep_counts.shape[0]
    slots = experts // exp_count * CAP
    longest = tokens * ctx_count // 2
    back = min(ctx_count - 1, -(-(longest - 1) // tokens))
    pieces = 2
    part = columns // pieces
    vmem = pl.BlockSpec(memory_space=pltpu.VMEM)
    hbm = pl.BlockSpec(memory_space=pl.ANY)
    bf16, f32 = jnp.bfloat16, jnp.float32
    dma = pltpu.SemaphoreType.DMA
    n = ctx_count
    stream = residual[0]
    if columns % 128:
        stream = stream.reshape(half, ctx_count, columns).transpose(1, 0, 2)
    out = pl.pallas_call(
        functools.partial(kernel, (ctx_count, exp_count, back, pieces)),
        out_shape=jax.ShapeDtypeStruct((exp_count, slots // CAP, CAP, width), bf16),
        in_specs=[vmem, vmem, vmem, vmem, hbm, hbm, vmem, vmem, vmem, vmem],
        out_specs=vmem,
        scratch_shapes=[
            pltpu.VMEM((groups, 2, tokens, size), bf16),
            pltpu.VMEM((groups, back, 2, tokens, size), bf16),
            pltpu.VMEM((1, width), f32),
            pltpu.VMEM((slots, 128), f32),
            pltpu.VMEM((back, 1, tokens), jnp.int32),
            pltpu.VMEM((n, groups, tokens, features // groups), bf16),
            pltpu.VMEM((features, columns), bf16),
            pltpu.VMEM((n, half, columns), bf16),
            pltpu.VMEM((n, pieces, 2, half, part), f32),
            pltpu.VMEM((n, pieces, half, part), bf16),
            pltpu.VMEM((n, pieces, half, part), bf16),
            pltpu.VMEM((n, pieces, half, part), bf16),
            pltpu.VMEM((n, pieces, half, part), bf16),
            pltpu.VMEM((exp_count - 1, n, pieces, slots, part), bf16),
            pltpu.VMEM((exp_count, n, pieces, slots, part), bf16),
            dma((1 + n,)),
            dma((groups, back)),
            dma((groups, back)),
            dma((back,)),
            dma((back,)),
            dma((n, groups)),
            dma((n, groups)),
            dma((n, groups)),
            dma((n, pieces)),
            dma((n, pieces)),
            dma((n, pieces)),
            dma((n, pieces)),
            dma((exp_count - 1, n, pieces)),
            dma((exp_count, n, pieces)),
        ],
        compiler_params=pltpu.CompilerParams(collective_id=0, has_side_effects=True),
    )(
        queries[0].transpose(1, 0, 2),
        key_states[0],
        values[0],
        doc_ids,
        stream,
        out_proj,
        norm_gain.reshape(width // 128, 128),
        router.T,
        expert_ids.reshape(1, half),
        keep_counts.reshape(1, experts),
    )
    return out


def solution(mesh):
    placed = (
        P(("groups", "exp"), "ctx", "tp", None),
        P(("groups", "exp"), "ctx", "tp", None),
        P(("groups", "exp"), "ctx", "tp", None),
        P(("groups", "exp"), "ctx"),
        P(("groups", "exp"), ("ctx", "tp"), None),
        P("tp", "ctx"),
        P(),
        P(None, "exp"),
        P(("groups", "exp"), ("ctx", "tp"), None),
        P("groups"),
    )
    return jax.shard_map(
        on_device,
        mesh=mesh,
        in_specs=placed,
        out_specs=P(("groups", "ctx", "tp"), "exp", None, None),
        check_vma=False,
    )
```

profile of v0, /device:TPU:0, one launch (start us, length us, event | category | flops | bytes accessed | tf_op | source)
XLA Modules:
  0.0 61.8 jit_solution(2850476673164226288)
XLA Ops:
  0.0 58.5 %shard_map.100 = bf16[2,32,2,5120]{3,2,1,0:T(2,128)(2,1)} custom-call(bf16[10,128,128]{2,1,0:T(8,128)(2,1)} %bitcast.11, bf16[128,2,128]{2,1,0:T(2,128)(2,1)} %bitcast.13, bf16[128,2,128]{2,1,0:T(2,128)(2,1)} %bitcast.14, s32[1,128]{1,0:T(1,128)} %doc_ref.1, bf16[64,5120]{1,0:T(8,128)(2,1)} %bitcast.10, bf16[1280,1280]{1,0:T(8,128)(2,1)} %weight_hbm.1, ...), custom_call_target="tpu_custom_call" | custom-call | tf_op jit(solution)/shard_map/pallas_call | solution.py:496
  58.5 3.3 %copy.12 = bf16[2,32,2,5120]{3,2,1,0:T(2,128)(2,1)} copy(bf16[2,32,2,5120]{3,2,1,0:T(2,128)(2,1)} %shard_map.100) | data formatting | bytes 2621440
where the time goes:
time: 62 us; the launch traced here: 61.8 us
  Pallas kernels  58.5 us (94%)
  local copies, waits for them, and re-layouts  3.27 us (5%)
    pallas_call x1, Pallas kernels, on_device(): pl.pallas_call(functools.partial(kernel, (ctx_count, exp_count, back, pie...  58.5 us
    unnamed x1, local copies, waits for them, and re-layouts  3.27 us

commit v1 on v0

v1 whole, which is shorter than its diff:
```python
import functools
import math

import jax
import jax.numpy as jnp
from jax import lax
from jax.experimental import pallas as pl
from jax.experimental.pallas import tpu as pltpu
from jax.sharding import PartitionSpec as P

CAP = 2
EPSILON = 1e-05
MESH = pl.DeviceIdType.MESH


def kernel(
    sizes,
    q_hbm,
    key_hbm,
    value_hbm,
    doc_hbm,
    residual_hbm,
    weight_hbm,
    gain_hbm,
    router_hbm,
    ids_hbm,
    keep_hbm,
    slot_in,
    scale_ref,
    q_ref,
    key_ref,
    value_ref,
    doc_ref,
    gain_ref,
    router_ref,
    ids_ref,
    keep_ref,
    kv_out,
    kv_in,
    routed,
    tally,
    logits,
    doc_in,
    attn,
    weight,
    residual,
    product,
    part_out,
    part_in,
    res_out,
    res_in,
    slot_out,
    load_sem,
    kv_send,
    kv_recv,
    doc_send,
    doc_recv,
    right_send,
    left_send,
    attn_recv,
    part_send,
    part_recv,
    res_send,
    res_recv,
    slot_send,
    slot_recv,
):
    ctx_count, exp_count, back, pieces = sizes
    heads, tokens, size = q_ref.shape
    groups = kv_out.shape[0]
    ratio = heads // groups
    half = tokens // 2
    columns = weight.shape[1]
    depth = weight.shape[0] // groups
    slots = slot_out.shape[3]
    part = columns // pieces
    width = columns * ctx_count
    aligned = part % 128 == 0
    me = lax.axis_index("ctx")
    mine = lax.axis_index("exp")
    core = lax.axis_index("tp")

    barrier = pltpu.get_barrier_semaphore()
    for shift in range(1, ctx_count):
        pl.semaphore_signal(
            barrier,
            inc=1,
            device_id={"ctx": lax.rem(me + shift, ctx_count)},
            device_id_type=MESH,
        )
    for shift in range(1, exp_count):
        pl.semaphore_signal(
            barrier,
            inc=1,
            device_id={"exp": lax.rem(mine + shift, exp_count)},
            device_id_type=MESH,
        )
    pl.semaphore_signal(barrier, inc=1, device_id={"tp": 1 - core}, device_id_type=MESH)

    loads = {}

    def load(name, source, target):
        loads[name] = pltpu.make_async_copy(source, target, load_sem.at[len(loads)])
        loads[name].start()

    load("key", key_hbm, key_ref)
    load("value", value_hbm, value_ref)
    load("doc", doc_hbm, doc_ref)
    load("query", q_hbm, q_ref)
    load("ids", ids_hbm, ids_ref)
    load("keep", keep_hbm, keep_ref)
    load("gain", gain_hbm, gain_ref)
    load("router", router_hbm, router_ref)
    load("weight", weight_hbm, weight)
    for block in range(ctx_count):
        there = slice(block * columns, (block + 1) * columns)
        load(
            block,
            residual_hbm.at[:, there] if columns % 128 == 0 else residual_hbm.at[block],
            residual.at[block],
        )

    loads["key"].wait()
    loads["value"].wait()
    for group in range(groups):
        kv_out[group, 0] = key_ref[:, group, :]
        kv_out[group, 1] = value_ref[:, group, :]
    loads["doc"].wait()

    pl.semaphore_wait(barrier, ctx_count + exp_count - 1)

    def kv_copy(group, shift):
        return pltpu.make_async_remote_copy(
            src_ref=kv_out.at[group] if shift == 1 else kv_in.at[group, shift - 2],
            dst_ref=kv_in.at[group, shift - 1],
            send_sem=kv_send.at[group, shift - 1],
            recv_sem=kv_recv.at[group, shift - 1],
            device_id={"ctx": lax.rem(me + 1, ctx_count)},
            device_id_type=MESH,
        )

    def doc_copy(shift):
        return pltpu.make_async_remote_copy(
            src_ref=doc_ref,
            dst_ref=doc_in.at[shift - 1],
            send_sem=doc_send.at[shift - 1],
            recv_sem=doc_recv.at[shift - 1],
            device_id={"ctx": lax.rem(me + shift, ctx_count)},
            device_id_type=MESH,
        )

    @pl.when(me < ctx_count - 1)
    def _():
        for group in range(groups):
            kv_copy(group, 1).start()

    for shift in range(1, back + 1):

        @pl.when(me + shift < ctx_count)
        def _(shift=shift):
            doc_copy(shift).start()

    for shift in range(1, back + 1):

        @pl.when(me < shift)
        def _(shift=shift):
            doc_in[shift - 1] = jnp.full(doc_in.shape[1:], -1, jnp.int32)
            for group in range(groups):
                kv_in[group, shift - 1] = jnp.zeros(kv_in.shape[2:], kv_in.dtype)

    def kv_arrive(group, shift):
        @pl.when(me >= shift)
        def _():
            kv_copy(group, shift).wait_recv()
            if shift < back:

                @pl.when(me < ctx_count - 1)
                def _():
                    kv_copy(group, shift + 1).start()

    loads["ids"].wait()
    loads["keep"].wait()
    row = lax.broadcasted_iota(jnp.int32, (half, half), 0)
    lane = lax.broadcasted_iota(jnp.int32, (half, half), 1)
    ids_row = ids_ref[...]
    ids_column = jnp.sum(jnp.where(row == lane, ids_row, 0), axis=1, keepdims=True)
    ranking = jnp.sum(
        jnp.where((ids_column == ids_row) & (row < lane), 1, 0), axis=0, keepdims=True
    )
    experts = keep_ref.shape[1]
    square_row = lax.broadcasted_iota(jnp.int32, (experts, experts), 0)
    square_lane = lax.broadcasted_iota(jnp.int32, (experts, experts), 1)
    keep_column = jnp.sum(
        jnp.where(square_row == square_lane, keep_ref[...], 0), axis=1, keepdims=True
    )
    expert_row = lax.broadcasted_iota(jnp.int32, (experts, half), 0)
    limits = jnp.sum(jnp.where(expert_row == ids_row, keep_column, 0), axis=0, keepdims=True)
    target = jnp.where(ranking < limits, ids_row * CAP + ranking, -1)
    slot_row = lax.broadcasted_iota(jnp.int32, (slots, half), 0)

    for shift in range(1, back):
        for group in range(groups):
            kv_arrive(group, shift)

    for shift in range(1, back + 1):

        @pl.when(me >= shift)
        def _(shift=shift):
            doc_copy(shift).wait_recv()

    square = lax.broadcasted_iota(jnp.int32, (tokens, tokens), 0)
    across = lax.broadcasted_iota(jnp.int32, (tokens, tokens), 1)
    doc_row = doc_ref[...]
    doc_column = jnp.sum(jnp.where(square == across, doc_row, 0), axis=1, keepdims=True)
    allowed = [(across <= square) & (doc_row == doc_column)]
    for shift in range(1, back + 1):
        allowed.append(doc_in[shift - 1] == doc_column)
    allowed = jnp.concatenate(
        [jnp.where(piece, 1.0, 0.0) for piece in allowed], axis=1
    )
    allowed = allowed > 0.5
    scale = 1.0 / math.sqrt(size)
    loads["query"].wait()

    def attn_copy(block, group, rightward):
        to = me + 1 if rightward else me - 1
        sends = right_send if rightward else left_send
        return pltpu.make_async_remote_copy(
            src_ref=attn.at[block, group],
            dst_ref=attn.at[block, group],
            send_sem=sends.at[block, group],
            recv_sem=attn_recv.at[block, group],
            device_id={"ctx": lax.rem(to + ctx_count, ctx_count)},
            device_id_type=MESH,
        )

    for group in range(groups):
        if back:
            kv_arrive(group, back)
        keys = jnp.concatenate(
            [kv_out[group, 0]] + [kv_in[group, shift, 0] for shift in range(back)], axis=0
        )
        vals = jnp.concatenate(
            [kv_out[group, 1]] + [kv_in[group, shift, 1] for shift in range(back)], axis=0
        )
        for head in range(ratio):
            scores = (
                lax.dot_general(
                    q_ref[group * ratio + head],
                    keys,
                    (((1,), (1,)), ((), ())),
                    preferred_element_type=jnp.float32,
                )
                * scale
            )
            masked = jnp.where(allowed, scores, -1e30)
            highest = jnp.max(masked, axis=1, keepdims=True)
            weights = jnp.where(allowed, jnp.exp(masked - highest), 0.0)
            totals = jnp.sum(weights, axis=1, keepdims=True)
            mixed = jnp.dot(weights.astype(jnp.bfloat16), vals, preferred_element_type=jnp.float32)
            attn[me, group, :, head * size : (head + 1) * size] = (mixed / totals).astype(
                jnp.bfloat16
            )

        @pl.when(me < ctx_count - 1)
        def _(group=group):
            attn_copy(me, group, True).start()

        @pl.when(me > 0)
        def _(group=group):
            attn_copy(me, group, False).start()

    def part_copy(block, piece):
        return pltpu.make_async_remote_copy(
            src_ref=part_out.at[block, piece],
            dst_ref=part_in.at[block, piece],
            send_sem=part_send.at[block, piece],
            recv_sem=part_recv.at[block, piece],
            device_id={"tp": 1 - core},
            device_id_type=MESH,
        )

    def res_copy(block, peer, piece):
        return pltpu.make_async_remote_copy(
            src_ref=res_out.at[block, piece],
            dst_ref=res_in.at[me, piece],
            send_sem=res_send.at[block, piece],
            recv_sem=res_recv.at[peer, piece],
            device_id={"ctx": block},
            device_id_type=MESH,
        )

    def slot_at(peer, block, piece):
        if aligned:
            first = pl.multiple_of(block * columns + piece * part, 128)
            return slot_in.at[peer, :, pl.ds(first, part)]
        return slot_in.at[peer, block, piece]

    def slot_copy(shift, block, peer, piece):
        return pltpu.make_async_remote_copy(
            src_ref=slot_out.at[shift - 1, block, piece],
            dst_ref=slot_at(mine, block, piece),
            send_sem=slot_send.at[shift - 1, block, piece],
            recv_sem=slot_recv.at[peer, block, piece],
            device_id={"exp": lax.rem(mine + shift, exp_count)},
            device_id_type=MESH,
        )

    def project(block, group):
        for piece in range(pieces):
            there = slice(piece * part, (piece + 1) * part)
            term = jnp.dot(
                attn[block, group],
                weight[group * depth : (group + 1) * depth, there],
                preferred_element_type=jnp.float32,
            )
            for side in range(2):
                rows = term[side * half : (side + 1) * half]
                if group:
                    rows = rows + product[block, piece, side]
                product[block, piece, side] = rows
            if group == groups - 1:
                part_out[block, piece] = product[block, piece, 1 - core].astype(jnp.bfloat16)
                part_copy(block, piece).start()

    def finish(block, piece):
        part_copy(block, piece).wait_recv()
        return (
            product[block, piece, core] + part_in[block, piece].astype(jnp.float32)
        ).astype(jnp.bfloat16)

    def send(block):
        for piece in range(pieces):
            res_copy(block, me, piece).start()

    def send_all(count, sign):
        def body(distance, carry):
            send(me + sign * distance)
            return carry

        lax.fori_loop(1, count + 1, body, 0)

    def place(block, piece):
        hidden = (
            residual[block, :, piece * part : (piece + 1) * part].astype(jnp.float32)
            + res_in[block, piece].astype(jnp.float32)
        ).astype(jnp.bfloat16)
        for shift in (*range(1, exp_count), 0):
            peer = lax.rem(mine + shift, exp_count)
            table = (slot_row + peer * slots == target).astype(jnp.bfloat16)
            chosen = jnp.dot(table, hidden, preferred_element_type=jnp.float32).astype(
                jnp.bfloat16
            )
            if shift == 0:
                slot_at(mine, block, piece)[...] = chosen
            else:
                slot_out[shift - 1, block, piece] = chosen
                slot_copy(shift, block, mine, piece).start()

    def absorb(shift, block):
        peer = lax.rem(mine + shift, exp_count)
        for piece in range(pieces):
            if shift:
                slot_copy(1, block, peer, piece).wait_recv()
            hidden = slot_at(peer, block, piece)[...]
            if aligned:
                first = pl.multiple_of(block * columns + piece * part, 128)
                columns_here = routed[:, pl.ds(first, part)]
            else:
                columns_here = routed[block, piece]
            logits[shift] += lax.dot_general(
                hidden,
                columns_here,
                (((1,), (1,)), ((), ())),
                preferred_element_type=jnp.float32,
            )
            wide = hidden.astype(jnp.float32)
            wide = wide * wide
            if aligned:
                total = wide[:, :128]
                for first in range(128, part, 128):
                    total = total + wide[:, first : first + 128]
                tally[shift] += total
            else:
                tally[shift, :, :1] += jnp.sum(wide, axis=1, keepdims=True)

    loads["weight"].wait()
    for group in range(groups):
        project(me, group)

    loads["gain"].wait()
    loads["router"].wait()
    wide = gain_ref[...].astype(jnp.float32)
    for line in range(wide.shape[0]):
        there = slice(line * 128, (line + 1) * 128)
        router_ref[:, there] = (
            router_ref[:, there].astype(jnp.float32) * wide[line : line + 1]
        ).astype(jnp.bfloat16)
    if not aligned:
        for block in range(ctx_count):
            for piece in range(pieces):
                first = block * columns + piece * part
                routed[block, piece] = router_ref[:, first : first + part]
    else:
        routed = router_ref
    tally[...] = jnp.zeros_like(tally)
    logits[...] = jnp.zeros_like(logits)
    for block in range(ctx_count):
        loads[block].wait()

    rest = ctx_count - 1 - me

    def step(distance, carry):
        left, right = me - distance, me + distance
        has_left, has_right = left >= 0, right < ctx_count

        for group in range(groups):

            @pl.when(has_left)
            def _():
                attn_copy(left, group, True).wait_recv()

                @pl.when(me < ctx_count - 1)
                def _():
                    attn_copy(left, group, True).start()

            @pl.when(has_right)
            def _():
                attn_copy(right, group, False).wait_recv()

                @pl.when(me > 0)
                def _():
                    attn_copy(right, group, False).start()

            for block, has in ((left, has_left), (right, has_right)):

                @pl.when(has)
                def _(block=block):
                    project(block, group)

        for block, has in ((left, has_left), (right, has_right)):

            @pl.when(has)
            def _(block=block):
                for piece in range(pieces):
                    res_out[block, piece] = finish(block, piece)

        @pl.when(has_right & (distance > me))
        def _():
            send(right)

        @pl.when(distance == me)
        def _():
            send_all(jnp.minimum(me, rest), 1)

        @pl.when(has_left & (distance > rest))
        def _():
            send(left)

        @pl.when(distance == rest)
        def _():
            send_all(jnp.minimum(me, rest), -1)

        @pl.when(distance == 1)
        def _():
            for piece in range(pieces):
                res_in[me, piece] = finish(me, piece)
                place(me, piece)
            absorb(0, me)

        return carry

    lax.fori_loop(1, ctx_count, step, 0)

    def settle(distance, carry):
        for block, has in (
            (me - distance, (me >= distance) & (distance < ctx_count)),
            (me + distance, me + distance < ctx_count),
        ):

            @pl.when(has)
            def _(block=block):
                for piece in range(pieces):
                    res_copy(me, block, piece).wait_recv()
                    place(block, piece)
                absorb(0, block)

        last = distance - 1
        for block, has in (
            (me - last, me >= last),
            (me + last, (me + last < ctx_count) & (last > 0)),
        ):

            @pl.when(has)
            def _(block=block):
                for shift in range(1, exp_count):
                    absorb(shift, block)

        return carry

    lax.fori_loop(1, ctx_count + 1, settle, 0)

    spread = lax.broadcasted_iota(jnp.int32, logits.shape[1:], 0) // CAP
    expert = lax.broadcasted_iota(jnp.int32, logits.shape[1:], 1)
    for shift in range(exp_count):
        peer = lax.rem(mine + shift, exp_count)
        power = tally[shift] if aligned else tally[shift, :, :1]
        power = jnp.sum(power, axis=1, keepdims=True) / width
        factor = lax.rsqrt(power + EPSILON)
        logit = jnp.sum(jnp.where(spread == expert, logits[shift], 0.0), axis=1, keepdims=True)
        gate = jax.nn.sigmoid(logit * factor)
        scale_ref[peer] = jnp.broadcast_to(gate * factor, scale_ref.shape[1:])

    @pl.when(me < ctx_count - 1)
    def _():
        for group in range(groups):
            kv_copy(group, 1).wait_send()
            for shift in range(1, back):

                @pl.when(me >= shift)
                def _(group=group, shift=shift):
                    kv_copy(group, shift + 1).wait_send()

    for shift in range(1, back + 1):

        @pl.when(me + shift < ctx_count)
        def _(shift=shift):
            doc_copy(shift).wait_send()

    def drain(block, carry):
        for piece in range(pieces):
            part_copy(block, piece).wait_send()
            for shift in range(1, exp_count):
                slot_copy(shift, block, mine, piece).wait_send()

        @pl.when(block != me)
        def _():
            for piece in range(pieces):
                res_copy(block, me, piece).wait_send()

        for group in range(groups):

            @pl.when((block <= me) & (me < ctx_count - 1))
            def _(group=group):
                attn_copy(block, group, True).wait_send()

            @pl.when((block >= me) & (me > 0))
            def _(group=group):
                attn_copy(block, group, False).wait_send()

        return carry

    lax.fori_loop(0, ctx_count, drain, 0)


def on_device(
    queries,
    key_states,
    values,
    doc_ids,
    residual,
    out_proj,
    norm_gain,
    router,
    expert_ids,
    keep_counts,
):
    tokens, heads, size = queries.shape[1:]
    groups = key_states.shape[2]
    ctx_count = lax.axis_size("ctx")
    exp_count = lax.axis_size("exp")
    features, columns = out_proj.shape
    half = residual.shape[1]
    width = residual.shape[2]
    experts = keep_counts.shape[0]
    owned = experts // exp_count
    slots = owned * CAP
    longest = tokens * ctx_count // 2
    back = min(ctx_count - 1, -(-(longest - 1) // tokens))
    pieces = columns // 256 if columns % 256 == 0 else 2
    part = columns // pieces
    aligned = part % 128 == 0
    vmem = pl.BlockSpec(memory_space=pltpu.VMEM)
    hbm = pl.BlockSpec(memory_space=pltpu.HBM)
    bf16, f32, i32 = jnp.bfloat16, jnp.float32, jnp.int32
    dma = pltpu.SemaphoreType.DMA
    n = ctx_count
    stream = residual[0]
    if columns % 128:
        stream = stream.reshape(half, ctx_count, columns).transpose(1, 0, 2)
    slot_shape = (exp_count, slots, width) if aligned else (exp_count, n, pieces, slots, part)
    chosen, scale = pl.pallas_call(
        functools.partial(kernel, (ctx_count, exp_count, back, pieces)),
        out_shape=(
            jax.ShapeDtypeStruct(slot_shape, bf16),
            jax.ShapeDtypeStruct((exp_count, slots, 128), f32),
        ),
        in_specs=[hbm] * 10,
        out_specs=(vmem, vmem),
        scratch_shapes=[
            pltpu.VMEM((heads, tokens, size), bf16),
            pltpu.VMEM((tokens, groups, size), bf16),
            pltpu.VMEM((tokens, groups, size), bf16),
            pltpu.VMEM((1, tokens), i32),
            pltpu.VMEM((width // 128, 128), bf16),
            pltpu.VMEM((owned, width), bf16),
            pltpu.VMEM((1, half), i32),
            pltpu.VMEM((1, experts), i32),
            pltpu.VMEM((groups, 2, tokens, size), bf16),
            pltpu.VMEM((groups, back, 2, tokens, size), bf16),
            pltpu.VMEM((8, 128) if aligned else (n, pieces, owned, part), bf16),
            pltpu.VMEM((exp_count, slots, 128), f32),
            pltpu.VMEM((exp_count, slots, owned), f32),
            pltpu.VMEM((back, 1, tokens), i32),
            pltpu.VMEM((n, groups, tokens, features // groups), bf16),
            pltpu.VMEM((features, columns), bf16),
            pltpu.VMEM((n, half, columns), bf16),
            pltpu.VMEM((n, pieces, 2, half, part), f32),
            pltpu.VMEM((n, pieces, half, part), bf16),
            pltpu.VMEM((n, pieces, half, part), bf16),
            pltpu.VMEM((n, pieces, half, part), bf16),
            pltpu.VMEM((n, pieces, half, part), bf16),
            pltpu.VMEM((exp_count - 1, n, pieces, slots, part), bf16),
            dma((9 + n,)),
            dma((groups, back)),
            dma((groups, back)),
            dma((back,)),
            dma((back,)),
            dma((n, groups)),
            dma((n, groups)),
            dma((n, groups)),
            dma((n, pieces)),
            dma((n, pieces)),
            dma((n, pieces)),
            dma((n, pieces)),
            dma((exp_count - 1, n, pieces)),
            dma((exp_count, n, pieces)),
        ],
        compiler_params=pltpu.CompilerParams(
            collective_id=0, has_side_effects=True, vmem_limit_bytes=40 << 20
        ),
    )(
        *(
            pltpu.with_memory_space_constraint(operand, pltpu.HBM)
            for operand in (
                queries[0].transpose(1, 0, 2),
                key_states[0],
                values[0],
                doc_ids,
                stream,
                out_proj,
                norm_gain.reshape(width // 128, 128),
                router.T,
                expert_ids.reshape(1, half),
                keep_counts.reshape(1, experts),
            )
        )
    )
    if not aligned:
        chosen = chosen.transpose(0, 3, 1, 2, 4).reshape(exp_count, slots, width)
    scaled = chosen.astype(f32) * scale[:, :, :1] * norm_gain.astype(f32)
    return scaled.astype(bf16).reshape(exp_count, owned, CAP, width)


def solution(mesh):
    placed = (
        P(("groups", "exp"), "ctx", "tp", None),
        P(("groups", "exp"), "ctx", "tp", None),
        P(("groups", "exp"), "ctx", "tp", None),
        P(("groups", "exp"), "ctx"),
        P(("groups", "exp"), ("ctx", "tp"), None),
        P("tp", "ctx"),
        P(),
        P(None, "exp"),
        P(("groups", "exp"), ("ctx", "tp"), None),
        P("groups"),
    )
    return jax.shard_map(
        on_device,
        mesh=mesh,
        in_specs=placed,
        out_specs=P(("groups", "ctx", "tp"), "exp", None, None),
        check_vma=False,
    )
```

time: 62 us -> 64.2 us (1.035)
  Pallas kernels: 58.5 us -> 61.4 us
  local copies, waits for them, and re-layouts: 3.27 us -> 1.45 us
  other arithmetic: 0 us -> 1.1 us
    unnamed x1 -> x0, local copies, waits for them, and re-layouts: 3.27 us -> none
    pallas_call x1, Pallas kernels: 58.5 us -> 61.4 us  [on_device(): pl.pallas_call(functools.partial(kernel, (ctx_count, exp_count, back, pie...]
    reshape x0 -> x1, local copies, waits for them, and re-layouts: none -> 1.36 us  [on_device(): return scaled.astype(bf16).reshape(exp_count, owned, CAP, width)]
    convert_element_type x0 -> x2, other arithmetic: none -> 1.1 us  [the longest x1 0.7 us: on_device(): scaled = chosen.astype(f32) * scale[:, :, :1] * norm_gain.astype(f32)]
where the time goes in v1:
time: 64.2 us; the launch traced here: 64 us
  Pallas kernels  61.4 us (96%)
  local copies, waits for them, and re-layouts  1.45 us (2%)
  other arithmetic  1.1 us (2%)
    pallas_call x1, Pallas kernels, on_device(): pl.pallas_call(functools.partial(kernel, (ctx_count, exp_count, back, pie...  61.4 us
    reshape x1, local copies, waits for them, and re-layouts, on_device(): return scaled.astype(bf16).reshape(exp_count, owned, CAP, width)  1.36 us

profile of v1, /device:TPU:0, one launch (start us, length us, event | category | flops | bytes accessed | tf_op | source)
XLA Modules:
  0.0 64.0 jit_solution(6369575879981879045)
XLA Ops:
  0.0 0.7 %convert_element_type.10 = f32[5120]{0:T(1024)S(1)} convert(bf16[5120]{0:T(1024)(128)(2,1)} %param.16) | non-fusion elementwise | flops 5120 | bytes 30720 | tf_op jit(solution)/shard_map/convert_element_type | solution.py:661
  0.7 61.4 %shard_map.100 = (bf16[2,64,5120]{2,1,0:T(8,128)(2,1)S(1)}, f32[2,64,128]{2,1,0:T(8,128)S(1)}) custom-call(bf16[10,128,128]{2,1,0:T(8,128)(2,1)} %bitcast.11, bf16[128,2,128]{2,1,0:T(2,128)(2,1)} %bitcast.13, bf16[128,2,128]{2,1,0:T(2,128)(2,1)} %bitcast.14, s32[1,128]{1,0:T(1,128)} %doc_hbm.1, bf16[64,5120]{1,0:T(8,128)(2,1)} %bitcast.10, ...), custom_call_target="tpu_custom_call" | custom-call | tf_op jit(solution)/shard_map/pallas_call | solution.py:592
  62.1 0.1 slice_reduce_fusion
  62.2 0.4 multiply_convert_fusion
  62.6 1.4 %reshape.16 = bf16[2,32,2,5120]{3,2,1,0:T(2,128)(2,1)} reshape(bf16[2,64,5120]{2,1,0:T(8,128)(2,1)S(1)} %multiply_convert_fusion) | data formatting | bytes 2621440 | tf_op jit(solution)/shard_map/reshape | solution.py:662

commit v2 on v1

--- a/solution.py
+++ b/solution.py
@@ -10,6 +10,9 @@
 
 CAP = 2
 EPSILON = 1e-05
+LAG = 0
+SLOT_LAG = 2
+WIDE = 5
 MESH = pl.DeviceIdType.MESH
 
 
@@ -27,6 +30,7 @@
     keep_hbm,
     slot_in,
     scale_ref,
+    gain_row,
     q_ref,
     key_ref,
     value_ref,
@@ -37,6 +41,9 @@
     keep_ref,
     kv_out,
     kv_in,
+    kv_next,
+    q_next,
+    doc_next,
     routed,
     tally,
     logits,
@@ -55,6 +62,8 @@
     kv_recv,
     doc_send,
     doc_recv,
+    next_send,
+    next_recv,
     right_send,
     left_send,
     attn_recv,
@@ -79,6 +88,7 @@
     me = lax.axis_index("ctx")
     mine = lax.axis_index("exp")
     core = lax.axis_index("tp")
+    rest = ctx_count - 1 - me
 
     barrier = pltpu.get_barrier_semaphore()
     for shift in range(1, ctx_count):
@@ -149,16 +159,45 @@
             device_id_type=MESH,
         )
 
+    def next_copy(source, target, index):
+        return pltpu.make_async_remote_copy(
+            src_ref=source,
+            dst_ref=target,
+            send_sem=next_send.at[index],
+            recv_sem=next_recv.at[index],
+            device_id={"ctx": lax.rem(me + ctx_count - 1, ctx_count)},
+            device_id_type=MESH,
+        )
+
+    def next_doc():
+        return next_copy(doc_ref, doc_next, 2 * groups)
+
+    def next_kv(group):
+        return next_copy(kv_out.at[group], kv_next.at[group], 2 * group)
+
+    def next_query(group):
+        these = pl.ds(group * ratio, ratio)
+        return next_copy(q_ref.at[these], q_next.at[these], 2 * group + 1)
+
+    for shift in range(1, back + 1):
+
+        @pl.when(me + shift < ctx_count)
+        def _(shift=shift):
+            doc_copy(shift).start()
+
     @pl.when(me < ctx_count - 1)
     def _():
         for group in range(groups):
             kv_copy(group, 1).start()
 
-    for shift in range(1, back + 1):
-
-        @pl.when(me + shift < ctx_count)
-        def _(shift=shift):
-            doc_copy(shift).start()
+    loads["query"].wait()
+
+    @pl.when(me > 0)
+    def _():
+        next_doc().start()
+        for group in range(groups):
+            next_kv(group).start()
+            next_query(group).start()
 
     for shift in range(1, back + 1):
 
@@ -210,17 +249,34 @@
 
     square = lax.broadcasted_iota(jnp.int32, (tokens, tokens), 0)
     across = lax.broadcasted_iota(jnp.int32, (tokens, tokens), 1)
-    doc_row = doc_ref[...]
-    doc_column = jnp.sum(jnp.where(square == across, doc_row, 0), axis=1, keepdims=True)
-    allowed = [(across <= square) & (doc_row == doc_column)]
-    for shift in range(1, back + 1):
-        allowed.append(doc_in[shift - 1] == doc_column)
-    allowed = jnp.concatenate(
-        [jnp.where(piece, 1.0, 0.0) for piece in allowed], axis=1
-    )
-    allowed = allowed > 0.5
     scale = 1.0 / math.sqrt(size)
-    loads["query"].wait()
+
+    def visible(doc_row, earlier):
+        doc_column = jnp.sum(jnp.where(square == across, doc_row, 0), axis=1, keepdims=True)
+        masks = [(across <= square) & (doc_row == doc_column)]
+        masks += [other == doc_column for other in earlier]
+        return jnp.concatenate([jnp.where(mask, 1.0, 0.0) for mask in masks], axis=1) > 0.5
+
+    def attend(block, group, allowed, query, pairs):
+        keys = jnp.concatenate([pair[0] for pair in pairs], axis=0)
+        vals = jnp.concatenate([pair[1] for pair in pairs], axis=0)
+        count = keys.shape[0]
+        stacked = query[group * ratio : (group + 1) * ratio].reshape(ratio * tokens, size)
+        scores = lax.dot_general(
+            stacked, keys, (((1,), (1,)), ((), ())), preferred_element_type=jnp.float32
+        ).reshape(ratio, tokens, count)
+        masked = jnp.where(allowed[None], scores * scale, -1e30)
+        highest = jnp.max(masked, axis=2, keepdims=True)
+        weights = jnp.exp(masked - highest)
+        totals = jnp.sum(weights, axis=2, keepdims=True)
+        mixed = jnp.dot(
+            weights.astype(jnp.bfloat16).reshape(ratio * tokens, count),
+            vals,
+            preferred_element_type=jnp.float32,
+        ).reshape(ratio, tokens, size)
+        mixed = (mixed / totals).astype(jnp.bfloat16)
+        for head in range(ratio):
+            attn[block, group, :, head * size : (head + 1) * size] = mixed[head]
 
     def attn_copy(block, group, rightward):
         to = me + 1 if rightward else me - 1
@@ -234,41 +290,91 @@
             device_id_type=MESH,
         )
 
+    allowed = visible(doc_ref[...], [doc_in[shift] for shift in range(back)])
     for group in range(groups):
         if back:
             kv_arrive(group, back)
-        keys = jnp.concatenate(
-            [kv_out[group, 0]] + [kv_in[group, shift, 0] for shift in range(back)], axis=0
-        )
-        vals = jnp.concatenate(
-            [kv_out[group, 1]] + [kv_in[group, shift, 1] for shift in range(back)], axis=0
-        )
-        for head in range(ratio):
-            scores = (
-                lax.dot_general(
-                    q_ref[group * ratio + head],
-                    keys,
-                    (((1,), (1,)), ((), ())),
-                    preferred_element_type=jnp.float32,
-                )
-                * scale
-            )
-            masked = jnp.where(allowed, scores, -1e30)
-            highest = jnp.max(masked, axis=1, keepdims=True)
-            weights = jnp.where(allowed, jnp.exp(masked - highest), 0.0)
-            totals = jnp.sum(weights, axis=1, keepdims=True)
-            mixed = jnp.dot(weights.astype(jnp.bfloat16), vals, preferred_element_type=jnp.float32)
-            attn[me, group, :, head * size : (head + 1) * size] = (mixed / totals).astype(
-                jnp.bfloat16
-            )
-
-        @pl.when(me < ctx_count - 1)
+        attend(
+            me,
+            group,
+            allowed,
+            q_ref,
+            [kv_out.at[group]] + [kv_in.at[group, shift] for shift in range(back)],
+        )
+        early = group < groups - 1
+
+        @pl.when((me < ctx_count - 1) & (early | (me == 0)))
         def _(group=group):
             attn_copy(me, group, True).start()
 
-        @pl.when(me > 0)
-        def _(group=group):
-            attn_copy(me, group, False).start()
+    def item(turn, count):
+        order = turn - 1
+        spot = jnp.where(count > 0, lax.rem(order, jnp.maximum(count, 1)), 0)
+        group = sum((order >= count * number).astype(jnp.int32) for number in range(1, groups))
+        group = group if groups > 1 else jnp.int32(0)
+        final = group == groups - 1
+        active = (turn >= 1) & (turn <= groups * count)
+        return group, jnp.where(final, count - spot, spot + 1), final, active
+
+    beyond = jnp.maximum(rest - 1, 0)
+
+    def from_left(turn):
+        group, far, final, active = item(turn, me)
+        block = me - far
+
+        @pl.when(active)
+        def _():
+            attn_copy(block, group, True).wait_recv()
+
+            @pl.when(me < ctx_count - 1)
+            def _():
+                attn_copy(block, group, True).start()
+
+                @pl.when(turn == groups * me)
+                def _():
+                    attn_copy(me, groups - 1, True).start()
+
+        return block, active & final
+
+    def from_right(turn):
+        group = lax.rem(turn - 1, groups)
+        block = me + 2 + (turn - 1) // groups
+        final, active = group == groups - 1, turn <= groups * beyond
+
+        @pl.when(active)
+        def _():
+            attn_copy(block, group, False).wait_recv()
+
+            @pl.when(me > 0)
+            def _():
+                attn_copy(block, group, False).start()
+
+        return block, active & final
+
+    from_left(1)
+
+    @pl.when(rest > 0)
+    def _():
+        next_doc().wait_recv()
+        allowed = visible(
+            doc_next[...],
+            ([doc_ref[...]] if back else []) + [doc_in[shift] for shift in range(back - 1)],
+        )
+        for group in range(groups):
+            next_kv(group).wait_recv()
+            next_query(group).wait_recv()
+            attend(
+                me + 1,
+                group,
+                allowed,
+                q_next,
+                [kv_next.at[group]]
+                + ([kv_out.at[group]] if back else [])
+                + [kv_in.at[group, shift] for shift in range(back - 1)],
+            )
+            @pl.when(me > 0)
+            def _(group=group):
+                attn_copy(me + 1, group, False).start()
 
     def part_copy(block, piece):
         return pltpu.make_async_remote_copy(
@@ -306,20 +412,22 @@
             device_id_type=MESH,
         )
 
-    def project(block, group):
-        for piece in range(pieces):
-            there = slice(piece * part, (piece + 1) * part)
-            term = jnp.dot(
-                attn[block, group],
-                weight[group * depth : (group + 1) * depth, there],
-                preferred_element_type=jnp.float32,
-            )
-            for side in range(2):
-                rows = term[side * half : (side + 1) * half]
-                if group:
-                    rows = rows + product[block, piece, side]
-                product[block, piece, side] = rows
-            if group == groups - 1:
+    def project(block):
+        for start in range(0, pieces, WIDE):
+            some = range(start, min(start + WIDE, pieces))
+            there = slice(start * part, (some[-1] + 1) * part)
+            total = None
+            for group in range(groups):
+                term = jnp.dot(
+                    attn[block, group],
+                    weight[group * depth : (group + 1) * depth, there],
+                    preferred_element_type=jnp.float32,
+                )
+                total = term if total is None else total + term
+            for piece in some:
+                here = slice((piece - start) * part, (piece - start + 1) * part)
+                product[block, piece, 0] = total[:half, here]
+                product[block, piece, 1] = total[half:, here]
                 part_out[block, piece] = product[block, piece, 1 - core].astype(jnp.bfloat16)
                 part_copy(block, piece).start()
 
@@ -332,13 +440,6 @@
     def send(block):
         for piece in range(pieces):
             res_copy(block, me, piece).start()
-
-    def send_all(count, sign):
-        def body(distance, carry):
-            send(me + sign * distance)
-            return carry
-
-        lax.fori_loop(1, count + 1, body, 0)
 
     def place(block, piece):
         hidden = (
@@ -385,14 +486,18 @@
                 tally[shift, :, :1] += jnp.sum(wide, axis=1, keepdims=True)
 
     loads["weight"].wait()
-    for group in range(groups):
-        project(me, group)
+    project(me)
+
+    @pl.when(rest > 0)
+    def _():
+        project(me + 1)
 
     loads["gain"].wait()
     loads["router"].wait()
     wide = gain_ref[...].astype(jnp.float32)
     for line in range(wide.shape[0]):
         there = slice(line * 128, (line + 1) * 128)
+        gain_row[:, there] = wide[line : line + 1]
         router_ref[:, there] = (
             router_ref[:, there].astype(jnp.float32) * wide[line : line + 1]
         ).astype(jnp.bfloat16)
@@ -408,97 +513,112 @@
     for block in range(ctx_count):
         loads[block].wait()
 
-    rest = ctx_count - 1 - me
-
-    def step(distance, carry):
-        left, right = me - distance, me + distance
-        has_left, has_right = left >= 0, right < ctx_count
-
-        for group in range(groups):
-
-            @pl.when(has_left)
-            def _():
-                attn_copy(left, group, True).wait_recv()
-
-                @pl.when(me < ctx_count - 1)
+    def due(source):
+        apart = jnp.abs(source - me)
+        base = groups * jnp.maximum(source, me) - apart + (apart + 1) // 2
+        first = groups * beyond + jnp.where(
+            source == ctx_count - 1, 1, jnp.where(source == 1, 2, 3)
+        )
+        after = jnp.where(me == 0, first, base + 1)
+        before = jnp.where(apart == 1, groups * me + 1, base + 4)
+        return jnp.where(source > me, after, before)
+
+    def reply(block, now):
+        for piece in range(pieces):
+            res_out[block, piece] = finish(block, piece)
+            if now is not None:
+
+                @pl.when(now)
+                def _(piece=piece):
+                    res_copy(block, me, piece).start()
+
+    def send(block):
+        for piece in range(pieces):
+            res_copy(block, me, piece).start()
+
+    def place_all(block):
+        for piece in range(pieces):
+            res_copy(me, block, piece).wait_recv()
+            if piece == 0:
+
+                @pl.when(
+                    ((me > 0) & (block > me + 1))
+                    | ((block == 0) & (me > 1) & (rest > 0))
+                )
                 def _():
-                    attn_copy(left, group, True).start()
-
-            @pl.when(has_right)
-            def _():
-                attn_copy(right, group, False).wait_recv()
-
-                @pl.when(me > 0)
-                def _():
-                    attn_copy(right, group, False).start()
-
-            for block, has in ((left, has_left), (right, has_right)):
-
-                @pl.when(has)
-                def _(block=block):
-                    project(block, group)
-
-        for block, has in ((left, has_left), (right, has_right)):
-
-            @pl.when(has)
-            def _(block=block):
-                for piece in range(pieces):
-                    res_out[block, piece] = finish(block, piece)
-
-        @pl.when(has_right & (distance > me))
-        def _():
-            send(right)
-
-        @pl.when(distance == me)
-        def _():
-            send_all(jnp.minimum(me, rest), 1)
-
-        @pl.when(has_left & (distance > rest))
-        def _():
-            send(left)
-
-        @pl.when(distance == rest)
-        def _():
-            send_all(jnp.minimum(me, rest), -1)
-
-        @pl.when(distance == 1)
+                    send(block)
+
+            place(block, piece)
+        absorb(0, block)
+
+    def step(turn, carry):
+        left, left_whole = from_left(turn + 1)
+        right, right_whole = from_right(turn)
+
+        @pl.when(turn == 1)
         def _():
             for piece in range(pieces):
                 res_in[me, piece] = finish(me, piece)
                 place(me, piece)
             absorb(0, me)
 
-        return carry
-
-    lax.fori_loop(1, ctx_count, step, 0)
-
-    def settle(distance, carry):
-        for block, has in (
-            (me - distance, (me >= distance) & (distance < ctx_count)),
-            (me + distance, me + distance < ctx_count),
-        ):
+            @pl.when(rest > 0)
+            def _():
+                reply(me + 1, None)
+
+        @pl.when((rest > 0) & (turn == jnp.maximum(groups * me - 1, 1)))
+        def _():
+            send(me + 1)
+
+        whole = ((left, left_whole), (right, right_whole))
+        for block, has in whole:
 
             @pl.when(has)
             def _(block=block):
-                for piece in range(pieces):
-                    res_copy(me, block, piece).wait_recv()
-                    place(block, piece)
-                absorb(0, block)
-
-        last = distance - 1
-        for block, has in (
-            (me - last, me >= last),
-            (me + last, (me + last < ctx_count) & (last > 0)),
-        ):
+                project(block)
+
+        prompt = (left < me - 1) & ((left > 0) | (rest == 0))
+        for (block, has), now in zip(whole, (prompt, None)):
 
             @pl.when(has)
-            def _(block=block):
+            def _(block=block, now=now):
+                reply(block, now)
+
+        @pl.when((me > 0) & (turn == jnp.maximum(jnp.maximum(groups * me - 1, groups * beyond), 1)))
+        def _():
+            send(me - 1)
+
+        @pl.when((me == 0) & (turn == groups * beyond))
+        def _():
+            def body(block, carry):
+                send(block)
+                return carry
+
+            lax.fori_loop(2, ctx_count, body, 0)
+
+        @pl.when(turn == 1 + SLOT_LAG)
+        def _():
+            for shift in range(1, exp_count):
+                absorb(shift, me)
+
+        def arrivals(source, carry):
+            when = due(source) + LAG
+
+            @pl.when((source != me) & (turn == when))
+            def _():
+                place_all(source)
+
+            @pl.when((source != me) & (turn == when + SLOT_LAG))
+            def _():
                 for shift in range(1, exp_count):
-                    absorb(shift, block)
-
+                    absorb(shift, source)
+
+            return carry
+
+        lax.fori_loop(0, ctx_count, arrivals, 0)
         return carry
 
-    lax.fori_loop(1, ctx_count + 1, settle, 0)
+    lax.fori_loop(1, groups * (ctx_count - 1) + 4 + LAG + SLOT_LAG, step, 0)
 
     spread = lax.broadcasted_iota(jnp.int32, logits.shape[1:], 0) // CAP
     expert = lax.broadcasted_iota(jnp.int32, logits.shape[1:], 1)
@@ -527,6 +647,13 @@
         def _(shift=shift):
             doc_copy(shift).wait_send()
 
+    @pl.when(me > 0)
+    def _():
+        next_doc().wait_send()
+        for group in range(groups):
+            next_kv(group).wait_send()
+            next_query(group).wait_send()
+
     def drain(block, carry):
         for piece in range(pieces):
             part_copy(block, piece).wait_send()
@@ -544,7 +671,7 @@
             def _(group=group):
                 attn_copy(block, group, True).wait_send()
 
-            @pl.when((block >= me) & (me > 0))
+            @pl.when((block > me) & (me > 0))
             def _(group=group):
                 attn_copy(block, group, False).wait_send()
 
@@ -589,14 +716,15 @@
     if columns % 128:
         stream = stream.reshape(half, ctx_count, columns).transpose(1, 0, 2)
     slot_shape = (exp_count, slots, width) if aligned else (exp_count, n, pieces, slots, part)
-    chosen, scale = pl.pallas_call(
+    chosen, scale, gain = pl.pallas_call(
         functools.partial(kernel, (ctx_count, exp_count, back, pieces)),
         out_shape=(
             jax.ShapeDtypeStruct(slot_shape, bf16),
             jax.ShapeDtypeStruct((exp_count, slots, 128), f32),
+            jax.ShapeDtypeStruct((1, width), f32),
         ),
         in_specs=[hbm] * 10,
-        out_specs=(vmem, vmem),
+        out_specs=(vmem, vmem, vmem),
         scratch_shapes=[
             pltpu.VMEM((heads, tokens, size), bf16),
             pltpu.VMEM((tokens, groups, size), bf16),
@@ -608,6 +736,9 @@
             pltpu.VMEM((1, experts), i32),
             pltpu.VMEM((groups, 2, tokens, size), bf16),
             pltpu.VMEM((groups, back, 2, tokens, size), bf16),
+            pltpu.VMEM((groups, 2, tokens, size), bf16),
+            pltpu.VMEM((heads, tokens, size), bf16),
+            pltpu.VMEM((1, tokens), i32),
             pltpu.VMEM((8, 128) if aligned else (n, pieces, owned, part), bf16),
             pltpu.VMEM((exp_count, slots, 128), f32),
             pltpu.VMEM((exp_count, slots, owned), f32),
@@ -626,6 +757,8 @@
             dma((groups, back)),
             dma((back,)),
             dma((back,)),
+            dma((2 * groups + 1,)),
+            dma((2 * groups + 1,)),
             dma((n, groups)),
             dma((n, groups)),
             dma((n, groups)),
@@ -658,7 +791,7 @@
     )
     if not aligned:
         chosen = chosen.transpose(0, 3, 1, 2, 4).reshape(exp_count, slots, width)
-    scaled = chosen.astype(f32) * scale[:, :, :1] * norm_gain.astype(f32)
+    scaled = chosen.astype(f32) * scale[:, :, :1] * gain
     return scaled.astype(bf16).reshape(exp_count, owned, CAP, width)
 
 

time: 64.2 us -> 53.8 us (0.84)
  the two profiles are of different devices: /device:TPU:0 before, /device:TPU:24 now
where the time goes in v2:
time: 53.8 us; the launch traced here: 53.7 us
  Pallas kernels  51.8 us (96%)
  local copies, waits for them, and re-layouts  1.45 us (3%)
    pallas_call x1, Pallas kernels, on_device(): pl.pallas_call(functools.partial(kernel, (ctx_count, exp_count, back, pie...  51.8 us
    reshape x1, local copies, waits for them, and re-layouts, on_device(): return scaled.astype(bf16).reshape(exp_count, owned, CAP, width)  1.36 us

profile of v2, /device:TPU:24, one launch (start us, length us, event | category | flops | bytes accessed | tf_op | source)
XLA Modules:
  0.0 53.7 jit_solution(4364221667871122126)
XLA Ops:
  0.0 51.8 %shard_map.100 = (bf16[2,64,5120]{2,1,0:T(8,128)(2,1)S(1)}, f32[2,64,128]{2,1,0:T(8,128)S(1)}, f32[1,5120]{1,0:T(1,128)S(1)}) custom-call(bf16[10,128,128]{2,1,0:T(8,128)(2,1)} %bitcast.13, bf16[128,2,128]{2,1,0:T(2,128)(2,1)} %bitcast.15, bf16[128,2,128]{2,1,0:T(2,128)(2,1)} %bitcast.16, s32[1,128]{1,0:T(1,128)} %doc_hbm.1, bf16[64,5120]{1,0:T(8,128)(2,1)} %bitcast.12, ...), custom_call_target="tpu_custom_call" | custom-call | tf_op jit(solution)/shard_map/pallas_call | solution.py:719
  51.8 0.1 slice_reduce_fusion
  51.9 0.4 multiply_convert_fusion
  52.3 1.4 %reshape.16 = bf16[2,32,2,5120]{3,2,1,0:T(2,128)(2,1)} reshape(bf16[2,64,5120]{2,1,0:T(8,128)(2,1)S(1)} %multiply_convert_fusion) | data formatting | bytes 2621440 | tf_op jit(solution)/shard_map/reshape | solution.py:795

commit v3 on v2

--- a/solution.py
+++ b/solution.py
@@ -10,8 +10,7 @@
 
 CAP = 2
 EPSILON = 1e-05
-LAG = 0
-SLOT_LAG = 2
+HOLD = 2
 WIDE = 5
 MESH = pl.DeviceIdType.MESH
 
@@ -89,6 +88,7 @@
     mine = lax.axis_index("exp")
     core = lax.axis_index("tp")
     rest = ctx_count - 1 - me
+    early = (rest == 0) & (me > 1)
 
     barrier = pltpu.get_barrier_semaphore()
     for shift in range(1, ctx_count):
@@ -139,13 +139,13 @@
 
     pl.semaphore_wait(barrier, ctx_count + exp_count - 1)
 
-    def kv_copy(group, shift):
+    def kv_copy(group, shift, hops=1):
         return pltpu.make_async_remote_copy(
-            src_ref=kv_out.at[group] if shift == 1 else kv_in.at[group, shift - 2],
+            src_ref=kv_out.at[group] if shift == hops else kv_in.at[group, shift - 2],
             dst_ref=kv_in.at[group, shift - 1],
             send_sem=kv_send.at[group, shift - 1],
             recv_sem=kv_recv.at[group, shift - 1],
-            device_id={"ctx": lax.rem(me + 1, ctx_count)},
+            device_id={"ctx": lax.rem(me + hops, ctx_count)},
             device_id_type=MESH,
         )
 
@@ -189,6 +189,11 @@
     def _():
         for group in range(groups):
             kv_copy(group, 1).start()
+            if back > 1 and group < groups - 1:
+
+                @pl.when(me == 0)
+                def _(group=group):
+                    kv_copy(group, 2, 2).start()
 
     loads["query"].wait()
 
@@ -213,7 +218,9 @@
             kv_copy(group, shift).wait_recv()
             if shift < back:
 
-                @pl.when(me < ctx_count - 1)
+                relayed = (me > 1) | (shift > 1) | (group == groups - 1)
+
+                @pl.when((me < ctx_count - 1) & relayed)
                 def _():
                     kv_copy(group, shift + 1).start()
 
@@ -236,10 +243,6 @@
     limits = jnp.sum(jnp.where(expert_row == ids_row, keep_column, 0), axis=0, keepdims=True)
     target = jnp.where(ranking < limits, ids_row * CAP + ranking, -1)
     slot_row = lax.broadcasted_iota(jnp.int32, (slots, half), 0)
-
-    for shift in range(1, back):
-        for group in range(groups):
-            kv_arrive(group, shift)
 
     for shift in range(1, back + 1):
 
@@ -291,7 +294,8 @@
         )
 
     allowed = visible(doc_ref[...], [doc_in[shift] for shift in range(back)])
-    for group in range(groups):
+
+    def attend_own(group):
         if back:
             kv_arrive(group, back)
         attend(
@@ -301,11 +305,20 @@
             q_ref,
             [kv_out.at[group]] + [kv_in.at[group, shift] for shift in range(back)],
         )
-        early = group < groups - 1
-
-        @pl.when((me < ctx_count - 1) & (early | (me == 0)))
-        def _(group=group):
+        soon = group < groups - 1
+
+        @pl.when((me < ctx_count - 1) & (soon | (me == 0) | (rest == 1)))
+        def _():
             attn_copy(me, group, True).start()
+
+    for group in range(groups - 1):
+        for shift in range(1, back):
+            kv_arrive(group, shift)
+        attend_own(group)
+
+    @pl.when(me == 0)
+    def _():
+        attend_own(groups - 1)
 
     def item(turn, count):
         order = turn - 1
@@ -317,10 +330,12 @@
         return group, jnp.where(final, count - spot, spot + 1), final, active
 
     beyond = jnp.maximum(rest - 1, 0)
+    skipped = jnp.where(early, 1, 0)
+    upstream = me - skipped
 
     def from_left(turn):
-        group, far, final, active = item(turn, me)
-        block = me - far
+        group, far, final, active = item(turn, upstream)
+        block = upstream - far
 
         @pl.when(active)
         def _():
@@ -330,7 +345,7 @@
             def _():
                 attn_copy(block, group, True).start()
 
-                @pl.when(turn == groups * me)
+                @pl.when((turn == groups * me) & (rest > 1))
                 def _():
                     attn_copy(me, groups - 1, True).start()
 
@@ -351,36 +366,48 @@
 
         return block, active & final
 
-    from_left(1)
-
-    @pl.when(rest > 0)
-    def _():
-        next_doc().wait_recv()
-        allowed = visible(
-            doc_next[...],
-            ([doc_ref[...]] if back else []) + [doc_in[shift] for shift in range(back - 1)],
-        )
-        for group in range(groups):
+    def attend_next(group):
+        @pl.when(rest > 0)
+        def _():
             next_kv(group).wait_recv()
             next_query(group).wait_recv()
             attend(
                 me + 1,
                 group,
-                allowed,
+                visible(
+                    doc_next[...],
+                    ([doc_ref[...]] if back else []) + [doc_in[shift] for shift in range(back - 1)],
+                ),
                 q_next,
                 [kv_next.at[group]]
                 + ([kv_out.at[group]] if back else [])
                 + [kv_in.at[group, shift] for shift in range(back - 1)],
             )
+
             @pl.when(me > 0)
-            def _(group=group):
+            def _():
                 attn_copy(me + 1, group, False).start()
+
+    @pl.when(rest > 0)
+    def _():
+        next_doc().wait_recv()
+
+    for group in range(groups - 1):
+        attend_next(group)
+    for shift in range(1, back):
+        kv_arrive(groups - 1, shift)
+    from_left(1)
+    attend_next(groups - 1)
+
+    @pl.when(me > 0)
+    def _():
+        attend_own(groups - 1)
 
     def part_copy(block, piece):
         return pltpu.make_async_remote_copy(
             src_ref=part_out.at[block, piece],
             dst_ref=part_in.at[block, piece],
-            send_sem=part_send.at[block, piece],
+            send_sem=part_send.at[0],
             recv_sem=part_recv.at[block, piece],
             device_id={"tp": 1 - core},
             device_id_type=MESH,
@@ -390,7 +417,7 @@
         return pltpu.make_async_remote_copy(
             src_ref=res_out.at[block, piece],
             dst_ref=res_in.at[me, piece],
-            send_sem=res_send.at[block, piece],
+            send_sem=res_send.at[0],
             recv_sem=res_recv.at[peer, piece],
             device_id={"ctx": block},
             device_id_type=MESH,
@@ -402,12 +429,12 @@
             return slot_in.at[peer, :, pl.ds(first, part)]
         return slot_in.at[peer, block, piece]
 
-    def slot_copy(shift, block, peer, piece):
+    def slot_copy(shift, block, index, piece):
         return pltpu.make_async_remote_copy(
             src_ref=slot_out.at[shift - 1, block, piece],
             dst_ref=slot_at(mine, block, piece),
-            send_sem=slot_send.at[shift - 1, block, piece],
-            recv_sem=slot_recv.at[peer, block, piece],
+            send_sem=slot_send.at[shift - 1],
+            recv_sem=slot_recv.at[index, block, piece],
             device_id={"exp": lax.rem(mine + shift, exp_count)},
             device_id_type=MESH,
         )
@@ -456,34 +483,33 @@
                 slot_at(mine, block, piece)[...] = chosen
             else:
                 slot_out[shift - 1, block, piece] = chosen
-                slot_copy(shift, block, mine, piece).start()
-
-    def absorb(shift, block):
+                slot_copy(shift, block, exp_count - shift - 1, piece).start()
+
+    def absorb(shift, block, piece):
         peer = lax.rem(mine + shift, exp_count)
-        for piece in range(pieces):
-            if shift:
-                slot_copy(1, block, peer, piece).wait_recv()
-            hidden = slot_at(peer, block, piece)[...]
-            if aligned:
-                first = pl.multiple_of(block * columns + piece * part, 128)
-                columns_here = routed[:, pl.ds(first, part)]
-            else:
-                columns_here = routed[block, piece]
-            logits[shift] += lax.dot_general(
-                hidden,
-                columns_here,
-                (((1,), (1,)), ((), ())),
-                preferred_element_type=jnp.float32,
-            )
-            wide = hidden.astype(jnp.float32)
-            wide = wide * wide
-            if aligned:
-                total = wide[:, :128]
-                for first in range(128, part, 128):
-                    total = total + wide[:, first : first + 128]
-                tally[shift] += total
-            else:
-                tally[shift, :, :1] += jnp.sum(wide, axis=1, keepdims=True)
+        if shift:
+            slot_copy(1, block, shift - 1, piece).wait_recv()
+        hidden = slot_at(peer, block, piece)[...]
+        if aligned:
+            first = pl.multiple_of(block * columns + piece * part, 128)
+            columns_here = routed[:, pl.ds(first, part)]
+        else:
+            columns_here = routed[block, piece]
+        logits[shift] += lax.dot_general(
+            hidden,
+            columns_here,
+            (((1,), (1,)), ((), ())),
+            preferred_element_type=jnp.float32,
+        )
+        wide = hidden.astype(jnp.float32)
+        wide = wide * wide
+        if aligned:
+            total = wide[:, :128]
+            for first in range(128, part, 128):
+                total = total + wide[:, first : first + 128]
+            tally[shift] += total
+        else:
+            tally[shift, :, :1] += jnp.sum(wide, axis=1, keepdims=True)
 
     loads["weight"].wait()
     project(me)
@@ -513,16 +539,6 @@
     for block in range(ctx_count):
         loads[block].wait()
 
-    def due(source):
-        apart = jnp.abs(source - me)
-        base = groups * jnp.maximum(source, me) - apart + (apart + 1) // 2
-        first = groups * beyond + jnp.where(
-            source == ctx_count - 1, 1, jnp.where(source == 1, 2, 3)
-        )
-        after = jnp.where(me == 0, first, base + 1)
-        before = jnp.where(apart == 1, groups * me + 1, base + 4)
-        return jnp.where(source > me, after, before)
-
     def reply(block, now):
         for piece in range(pieces):
             res_out[block, piece] = finish(block, piece)
@@ -536,39 +552,97 @@
         for piece in range(pieces):
             res_copy(block, me, piece).start()
 
-    def place_all(block):
+    def order(number):
+        inner = jnp.where(number <= rest, me + number, number - rest - 1)
+        inner = jnp.where(number == 0, me - 1, inner)
+        return jnp.where(me == 0, jnp.where(number == 0, 1, ctx_count - number), inner)
+
+    def send_far(start):
+        def body(number, carry):
+            send(ctx_count - 1 - number)
+            return carry
+
+        lax.fori_loop(start, beyond, body, 0)
+
+    def settle(number, before):
+        block = order(number)
         for piece in range(pieces):
             res_copy(me, block, piece).wait_recv()
             if piece == 0:
 
-                @pl.when(
-                    ((me > 0) & (block > me + 1))
-                    | ((block == 0) & (me > 1) & (rest > 0))
-                )
+                @pl.when((me == 0) & (number == 1))
                 def _():
-                    send(block)
+                    send(ctx_count - 1)
+
+                @pl.when(early & (number == 1))
+                def _():
+                    def body(block, carry):
+                        send(block)
+                        return carry
+
+                    lax.fori_loop(1, me - 1, body, 0)
+
+            if piece == min(HOLD, pieces - 1):
+
+                @pl.when((me == 0) & (number == 2))
+                def _():
+                    send_far(1)
 
             place(block, piece)
-        absorb(0, block)
+            absorb(0, block, piece)
+            for shift in range(1, exp_count):
+                absorb(shift, before, piece)
+
+        @pl.when((number == 0) & (me > 1) & (rest > 0))
+        def _():
+            send(0)
+
+        @pl.when((number == 1) & (me > 0))
+        def _():
+            send_far(0)
+
+        return block
+
+    last = jnp.maximum(groups * upstream - 1, groups * beyond)
+
+    late = (rest == 1) & (me > 1)
+
+    def own():
+        for piece in range(pieces):
+            res_in[me, piece] = finish(me, piece)
+            place(me, piece)
+            absorb(0, me, piece)
+
+        @pl.when(rest > 0)
+        def _():
+            reply(me + 1, None)
+
+        @pl.when((rest > 0) & jnp.logical_not(late))
+        def _():
+            send(me + 1)
+
+    @pl.when(early)
+    def _():
+        for group in range(groups):
+            attn_copy(me - 1, group, True).wait_recv()
+        project(me - 1)
+
+    @pl.when((me == 0) | (rest == 0))
+    def _():
+        own()
+
+    @pl.when(early)
+    def _():
+        reply(me - 1, None)
+        send(me - 1)
 
     def step(turn, carry):
         left, left_whole = from_left(turn + 1)
         right, right_whole = from_right(turn)
 
-        @pl.when(turn == 1)
-        def _():
-            for piece in range(pieces):
-                res_in[me, piece] = finish(me, piece)
-                place(me, piece)
-            absorb(0, me)
-
-            @pl.when(rest > 0)
-            def _():
-                reply(me + 1, None)
-
-        @pl.when((rest > 0) & (turn == jnp.maximum(groups * me - 1, 1)))
-        def _():
-            send(me + 1)
+        @pl.when((turn == 1) & (me > 0) & (rest > 0))
+        def _():
+            own()
 
         whole = ((left, left_whole), (right, right_whole))
         for block, has in whole:
@@ -577,48 +651,35 @@
             def _(block=block):
                 project(block)
 
-        prompt = (left < me - 1) & ((left > 0) | (rest == 0))
+        prompt = (left < me - 1) & ((left > 0) != early)
         for (block, has), now in zip(whole, (prompt, None)):
 
             @pl.when(has)
             def _(block=block, now=now):
                 reply(block, now)
 
-        @pl.when((me > 0) & (turn == jnp.maximum(jnp.maximum(groups * me - 1, groups * beyond), 1)))
-        def _():
-            send(me - 1)
-
-        @pl.when((me == 0) & (turn == groups * beyond))
-        def _():
-            def body(block, carry):
-                send(block)
-                return carry
-
-            lax.fori_loop(2, ctx_count, body, 0)
-
-        @pl.when(turn == 1 + SLOT_LAG)
-        def _():
-            for shift in range(1, exp_count):
-                absorb(shift, me)
-
-        def arrivals(source, carry):
-            when = due(source) + LAG
-
-            @pl.when((source != me) & (turn == when))
-            def _():
-                place_all(source)
-
-            @pl.when((source != me) & (turn == when + SLOT_LAG))
-            def _():
-                for shift in range(1, exp_count):
-                    absorb(shift, source)
-
-            return carry
-
-        lax.fori_loop(0, ctx_count, arrivals, 0)
+        @pl.when(late & (turn == groups * me - 2))
+        def _():
+            send(me + 1)
+
+        @pl.when(early & (turn == (groups - 1) * upstream))
+        def _():
+            settle(0, me)
+
         return carry
 
-    lax.fori_loop(1, groups * (ctx_count - 1) + 4 + LAG + SLOT_LAG, step, 0)
+    lax.fori_loop(1, jnp.maximum(last, 1) + 1, step, 0)
+
+    @pl.when((me > 0) & (rest > 0) | (me == 1))
+    def _():
+        send(me - 1)
+
+    block = lax.fori_loop(
+        jnp.where(early, 1, 0), ctx_count - 1, settle, jnp.where(early, me - 1, me)
+    )
+    for piece in range(pieces):
+        for shift in range(1, exp_count):
+            absorb(shift, block, piece)
 
     spread = lax.broadcasted_iota(jnp.int32, logits.shape[1:], 0) // CAP
     expert = lax.broadcasted_iota(jnp.int32, logits.shape[1:], 1)
@@ -635,9 +696,16 @@
     def _():
         for group in range(groups):
             kv_copy(group, 1).wait_send()
+            if back > 1 and group < groups - 1:
+
+                @pl.when(me == 0)
+                def _(group=group):
+                    kv_copy(group, 2, 2).wait_send()
+
             for shift in range(1, back):
-
-                @pl.when(me >= shift)
+                relayed = (me > 1) | (shift > 1) | (group == groups - 1)
+
+                @pl.when((me >= shift) & relayed)
                 def _(group=group, shift=shift):
                     kv_copy(group, shift + 1).wait_send()
 
@@ -654,17 +722,22 @@
             next_kv(group).wait_send()
             next_query(group).wait_send()
 
+    def sent(source, semaphore):
+        pltpu.make_async_remote_copy(
+            src_ref=source,
+            dst_ref=source,
+            send_sem=semaphore,
+            recv_sem=semaphore,
+            device_id={"tp": 1 - core},
+            device_id_type=MESH,
+        ).wait_send()
+
+    sent(part_out, part_send.at[0])
+    sent(res_out.at[pl.ds(0, ctx_count - 1)], res_send.at[0])
+    for shift in range(1, exp_count):
+        sent(slot_out.at[shift - 1], slot_send.at[shift - 1])
+
     def drain(block, carry):
-        for piece in range(pieces):
-            part_copy(block, piece).wait_send()
-            for shift in range(1, exp_count):
-                slot_copy(shift, block, mine, piece).wait_send()
-
-        @pl.when(block != me)
-        def _():
-            for piece in range(pieces):
-                res_copy(block, me, piece).wait_send()
-
         for group in range(groups):
 
             @pl.when((block <= me) & (me < ctx_count - 1))
@@ -762,12 +835,12 @@
             dma((n, groups)),
             dma((n, groups)),
             dma((n, groups)),
+            dma((1,)),
             dma((n, pieces)),
+            dma((1,)),
             dma((n, pieces)),
-            dma((n, pieces)),
-            dma((n, pieces)),
+            dma((exp_count - 1,)),
             dma((exp_count - 1, n, pieces)),
-            dma((exp_count, n, pieces)),
         ],
         compiler_params=pltpu.CompilerParams(
             collective_id=0, has_side_effects=True, vmem_limit_bytes=40 << 20

time: 53.8 us -> 52.6 us (0.978)
  Pallas kernels: 51.8 us -> 50.5 us
    pallas_call x1, Pallas kernels: 51.8 us -> 50.5 us  [on_device(): pl.pallas_call(functools.partial(kernel, (ctx_count, exp_count, back, pie...]
where the time goes in v3:
time: 52.6 us; the launch traced here: 52.3 us
  Pallas kernels  50.5 us (96%)
  local copies, waits for them, and re-layouts  1.45 us (3%)
    pallas_call x1, Pallas kernels, on_device(): pl.pallas_call(functools.partial(kernel, (ctx_count, exp_count, back, pie...  50.5 us
    reshape x1, local copies, waits for them, and re-layouts, on_device(): return scaled.astype(bf16).reshape(exp_count, owned, CAP, width)  1.36 us

profile of v3, /device:TPU:24, one launch (start us, length us, event | category | flops | bytes accessed | tf_op | source)
XLA Modules:
  0.0 52.3 jit_solution(16834816884086514124)
XLA Ops:
  0.0 50.5 %shard_map.100 = (bf16[2,64,5120]{2,1,0:T(8,128)(2,1)S(1)}, f32[2,64,128]{2,1,0:T(8,128)S(1)}, f32[1,5120]{1,0:T(1,128)S(1)}) custom-call(bf16[10,128,128]{2,1,0:T(8,128)(2,1)} %bitcast.13, bf16[128,2,128]{2,1,0:T(2,128)(2,1)} %bitcast.15, bf16[128,2,128]{2,1,0:T(2,128)(2,1)} %bitcast.16, s32[1,128]{1,0:T(1,128)} %doc_hbm.1, bf16[64,5120]{1,0:T(8,128)(2,1)} %bitcast.12, ...), custom_call_target="tpu_custom_call" | custom-call | tf_op jit(solution)/shard_map/pallas_call | solution.py:792
  50.5 0.1 slice_reduce_fusion
  50.6 0.4 multiply_convert_fusion
  51.0 1.4 %reshape.16 = bf16[2,32,2,5120]{3,2,1,0:T(2,128)(2,1)} reshape(bf16[2,64,5120]{2,1,0:T(8,128)(2,1)S(1)} %multiply_convert_fusion) | data formatting | bytes 2621440 | tf_op jit(solution)/shard_map/reshape | solution.py:868

commit v4 on v3

--- a/solution.py
+++ b/solution.py
@@ -10,7 +10,6 @@
 
 CAP = 2
 EPSILON = 1e-05
-HOLD = 2
 WIDE = 5
 MESH = pl.DeviceIdType.MESH
 
@@ -55,6 +54,7 @@
     part_in,
     res_out,
     res_in,
+    passing,
     slot_out,
     load_sem,
     kv_send,
@@ -70,6 +70,8 @@
     part_recv,
     res_send,
     res_recv,
+    pass_send,
+    pass_recv,
     slot_send,
     slot_recv,
 ):
@@ -423,6 +425,39 @@
             device_id_type=MESH,
         )
 
+    routes = ((1, ctx_count - 3), (-1, 2)) if ctx_count > 3 else ()
+
+    def pass_copy(side):
+        sign, source = routes[side]
+        return pltpu.make_async_remote_copy(
+            src_ref=res_out.at[source + 2 * sign],
+            dst_ref=passing.at[side],
+            send_sem=res_send.at[0],
+            recv_sem=pass_recv.at[side],
+            device_id={"ctx": source + sign},
+            device_id_type=MESH,
+        )
+
+    def onward_copy(side, piece):
+        sign, source = routes[side]
+        return pltpu.make_async_remote_copy(
+            src_ref=passing.at[side, piece],
+            dst_ref=res_in.at[source, piece],
+            send_sem=pass_send.at[side],
+            recv_sem=res_recv.at[source, piece],
+            device_id={"ctx": source + 2 * sign},
+            device_id_type=MESH,
+        )
+
+    def pass_on():
+        for side, (sign, source) in enumerate(routes):
+
+            @pl.when(me == source + sign)
+            def _(side=side):
+                pass_copy(side).wait_recv()
+                for piece in range(pieces):
+                    onward_copy(side, piece).start()
+
     def slot_at(peer, block, piece):
         if aligned:
             first = pl.multiple_of(block * columns + piece * part, 128)
@@ -548,6 +583,12 @@
                 def _(piece=piece):
                     res_copy(block, me, piece).start()
 
+        for side, (sign, source) in enumerate(routes):
+
+            @pl.when((me == source) & (block == source + 2 * sign))
+            def _(side=side):
+                pass_copy(side).start()
+
     def send(block):
         for piece in range(pieces):
             res_copy(block, me, piece).start()
@@ -557,12 +598,12 @@
         inner = jnp.where(number == 0, me - 1, inner)
         return jnp.where(me == 0, jnp.where(number == 0, 1, ctx_count - number), inner)
 
-    def send_far(start):
+    def send_far():
         def body(number, carry):
             send(ctx_count - 1 - number)
             return carry
 
-        lax.fori_loop(start, beyond, body, 0)
+        lax.fori_loop(0, beyond, body, 0)
 
     def settle(number, before):
         block = order(number)
@@ -572,34 +613,26 @@
 
                 @pl.when((me == 0) & (number == 1))
                 def _():
-                    send(ctx_count - 1)
-
-                @pl.when(early & (number == 1))
-                def _():
-                    def body(block, carry):
-                        send(block)
-                        return carry
-
-                    lax.fori_loop(1, me - 1, body, 0)
-
-            if piece == min(HOLD, pieces - 1):
-
-                @pl.when((me == 0) & (number == 2))
-                def _():
-                    send_far(1)
+                    send_far()
 
             place(block, piece)
             absorb(0, block, piece)
             for shift in range(1, exp_count):
                 absorb(shift, before, piece)
 
-        @pl.when((number == 0) & (me > 1) & (rest > 0))
+        direct = me > (2 if routes else 1)
+
+        @pl.when((number == 0) & direct & (rest > 0))
         def _():
             send(0)
 
-        @pl.when((number == 1) & (me > 0))
-        def _():
-            send_far(0)
+        @pl.when((number == 1) & (me > 0) & (rest > (2 if routes else 1)))
+        def _():
+            send_far()
+
+        @pl.when(number == 0)
+        def _():
+            pass_on()
 
         return block
 
@@ -651,7 +684,7 @@
             def _(block=block):
                 project(block)
 
-        prompt = (left < me - 1) & ((left > 0) != early)
+        prompt = (left < me - 1) & (early | (left > 0))
         for (block, has), now in zip(whole, (prompt, None)):
 
             @pl.when(has)
@@ -734,6 +767,12 @@
 
     sent(part_out, part_send.at[0])
     sent(res_out.at[pl.ds(0, ctx_count - 1)], res_send.at[0])
+    for side, (sign, source) in enumerate(routes):
+
+        @pl.when(me == source + sign)
+        def _(side=side):
+            sent(passing.at[side], pass_send.at[side])
+
     for shift in range(1, exp_count):
         sent(slot_out.at[shift - 1], slot_send.at[shift - 1])
 
@@ -824,6 +863,7 @@
             pltpu.VMEM((n, pieces, half, part), bf16),
             pltpu.VMEM((n, pieces, half, part), bf16),
             pltpu.VMEM((n, pieces, half, part), bf16),
+            pltpu.VMEM((2, pieces, half, part), bf16),
             pltpu.VMEM((exp_count - 1, n, pieces, slots, part), bf16),
             dma((9 + n,)),
             dma((groups, back)),
@@ -839,6 +879,8 @@
             dma((n, pieces)),
             dma((1,)),
             dma((n, pieces)),
+            dma((2,)),
+            dma((2,)),
             dma((exp_count - 1,)),
             dma((exp_count - 1, n, pieces)),
         ],

time: 52.6 us -> 51.5 us (0.979)
  Pallas kernels: 50.5 us -> 49 us
    pallas_call x1, Pallas kernels: 50.5 us -> 49 us  [on_device(): pl.pallas_call(functools.partial(kernel, (ctx_count, exp_count, back, pie...]
where the time goes in v4:
time: 51.5 us; the launch traced here: 50.9 us
  Pallas kernels  49 us (95%)
  local copies, waits for them, and re-layouts  1.45 us (3%)
    pallas_call x1, Pallas kernels, on_device(): pl.pallas_call(functools.partial(kernel, (ctx_count, exp_count, back, pie...  49 us
    reshape x1, local copies, waits for them, and re-layouts, on_device(): return scaled.astype(bf16).reshape(exp_count, owned, CAP, width)  1.36 us

profile of v4, /device:TPU:24, one launch (start us, length us, event | category | flops | bytes accessed | tf_op | source)
XLA Modules:
  0.0 50.9 jit_solution(7537391214086293323)
XLA Ops:
  0.0 49.0 %shard_map.100 = (bf16[2,64,5120]{2,1,0:T(8,128)(2,1)S(1)}, f32[2,64,128]{2,1,0:T(8,128)S(1)}, f32[1,5120]{1,0:T(1,128)S(1)}) custom-call(bf16[10,128,128]{2,1,0:T(8,128)(2,1)} %bitcast.13, bf16[128,2,128]{2,1,0:T(2,128)(2,1)} %bitcast.15, bf16[128,2,128]{2,1,0:T(2,128)(2,1)} %bitcast.16, s32[1,128]{1,0:T(1,128)} %doc_hbm.1, bf16[64,5120]{1,0:T(8,128)(2,1)} %bitcast.12, ...), custom_call_target="tpu_custom_call" | custom-call | tf_op jit(solution)/shard_map/pallas_call | solution.py:831
  49.0 0.1 slice_reduce_fusion
  49.1 0.4 multiply_convert_fusion
  49.5 1.4 %reshape.16 = bf16[2,32,2,5120]{3,2,1,0:T(2,128)(2,1)} reshape(bf16[2,64,5120]{2,1,0:T(8,128)(2,1)S(1)} %multiply_convert_fusion) | data formatting | bytes 2621440 | tf_op jit(solution)/shard_map/reshape | solution.py:910

commit v5 on v4

--- a/solution.py
+++ b/solution.py
@@ -313,9 +313,19 @@
         def _():
             attn_copy(me, group, True).start()
 
+    def kv_last():
+        for shift in range(1, back):
+            kv_arrive(groups - 1, shift)
+
     for group in range(groups - 1):
         for shift in range(1, back):
             kv_arrive(group, shift)
+        if group == 0:
+
+            @pl.when(me >= back)
+            def _():
+                kv_last()
+
         attend_own(group)
 
     @pl.when(me == 0)
@@ -396,8 +406,11 @@
 
     for group in range(groups - 1):
         attend_next(group)
-    for shift in range(1, back):
-        kv_arrive(groups - 1, shift)
+
+    @pl.when((me < back) | (groups == 1))
+    def _():
+        kv_last()
+
     from_left(1)
     attend_next(groups - 1)
 

time: 51.5 us -> 50.1 us (0.973)
  Pallas kernels: 49 us -> 47.6 us
    pallas_call x1, Pallas kernels: 49 us -> 47.6 us  [on_device(): pl.pallas_call(functools.partial(kernel, (ctx_count, exp_count, back, pie...]
where the time goes in v5:
time: 50.1 us; the launch traced here: 49.5 us
  Pallas kernels  47.6 us (95%)
  local copies, waits for them, and re-layouts  1.45 us (3%)
    pallas_call x1, Pallas kernels, on_device(): pl.pallas_call(functools.partial(kernel, (ctx_count, exp_count, back, pie...  47.6 us
    reshape x1, local copies, waits for them, and re-layouts, on_device(): return scaled.astype(bf16).reshape(exp_count, owned, CAP, width)  1.36 us

profile of v5, /device:TPU:24, one launch (start us, length us, event | category | flops | bytes accessed | tf_op | source)
XLA Modules:
  0.0 49.5 jit_solution(16087316707282551774)
XLA Ops:
  0.0 47.6 %shard_map.100 = (bf16[2,64,5120]{2,1,0:T(8,128)(2,1)S(1)}, f32[2,64,128]{2,1,0:T(8,128)S(1)}, f32[1,5120]{1,0:T(1,128)S(1)}) custom-call(bf16[10,128,128]{2,1,0:T(8,128)(2,1)} %bitcast.13, bf16[128,2,128]{2,1,0:T(2,128)(2,1)} %bitcast.15, bf16[128,2,128]{2,1,0:T(2,128)(2,1)} %bitcast.16, s32[1,128]{1,0:T(1,128)} %doc_hbm.1, bf16[64,5120]{1,0:T(8,128)(2,1)} %bitcast.12, ...), custom_call_target="tpu_custom_call" | custom-call | tf_op jit(solution)/shard_map/pallas_call | solution.py:844
  47.6 0.1 slice_reduce_fusion
  47.7 0.4 multiply_convert_fusion
  48.1 1.4 %reshape.16 = bf16[2,32,2,5120]{3,2,1,0:T(2,128)(2,1)} reshape(bf16[2,64,5120]{2,1,0:T(8,128)(2,1)S(1)} %multiply_convert_fusion) | data formatting | bytes 2621440 | tf_op jit(solution)/shard_map/reshape | solution.py:923

commit v6 on v5

--- a/solution.py
+++ b/solution.py
@@ -126,11 +126,11 @@
     load("weight", weight_hbm, weight)
     for block in range(ctx_count):
         there = slice(block * columns, (block + 1) * columns)
-        load(
-            block,
+        pltpu.make_async_copy(
             residual_hbm.at[:, there] if columns % 128 == 0 else residual_hbm.at[block],
             residual.at[block],
-        )
+            load_sem.at[len(loads)],
+        ).start()
 
     loads["key"].wait()
     loads["value"].wait()
@@ -289,7 +289,7 @@
         return pltpu.make_async_remote_copy(
             src_ref=attn.at[block, group],
             dst_ref=attn.at[block, group],
-            send_sem=sends.at[block, group],
+            send_sem=sends.at[0],
             recv_sem=attn_recv.at[block, group],
             device_id={"ctx": lax.rem(to + ctx_count, ctx_count)},
             device_id_type=MESH,
@@ -423,7 +423,7 @@
             src_ref=part_out.at[block, piece],
             dst_ref=part_in.at[block, piece],
             send_sem=part_send.at[0],
-            recv_sem=part_recv.at[block, piece],
+            recv_sem=part_recv.at[block],
             device_id={"tp": 1 - core},
             device_id_type=MESH,
         )
@@ -506,8 +506,17 @@
                 part_out[block, piece] = product[block, piece, 1 - core].astype(jnp.bfloat16)
                 part_copy(block, piece).start()
 
+    def parts_arrive(block):
+        pltpu.make_async_remote_copy(
+            src_ref=part_out.at[block],
+            dst_ref=part_in.at[block],
+            send_sem=part_send.at[0],
+            recv_sem=part_recv.at[block],
+            device_id={"tp": 1 - core},
+            device_id_type=MESH,
+        ).wait_recv()
+
     def finish(block, piece):
-        part_copy(block, piece).wait_recv()
         return (
             product[block, piece, core] + part_in[block, piece].astype(jnp.float32)
         ).astype(jnp.bfloat16)
@@ -584,10 +593,10 @@
         routed = router_ref
     tally[...] = jnp.zeros_like(tally)
     logits[...] = jnp.zeros_like(logits)
-    for block in range(ctx_count):
-        loads[block].wait()
+    pltpu.make_async_copy(residual, residual, load_sem.at[len(loads)]).wait()
 
     def reply(block, now):
+        parts_arrive(block)
         for piece in range(pieces):
             res_out[block, piece] = finish(block, piece)
             if now is not None:
@@ -654,6 +663,7 @@
     late = (rest == 1) & (me > 1)
 
     def own():
+        parts_arrive(me)
         for piece in range(pieces):
             res_in[me, piece] = finish(me, piece)
             place(me, piece)
@@ -729,6 +739,9 @@
 
     spread = lax.broadcasted_iota(jnp.int32, logits.shape[1:], 0) // CAP
     expert = lax.broadcasted_iota(jnp.int32, logits.shape[1:], 1)
+    slot_across = lax.broadcasted_iota(jnp.int32, (slots, slots), 0) == (
+        lax.broadcasted_iota(jnp.int32, (slots, slots), 1)
+    )
     for shift in range(exp_count):
         peer = lax.rem(mine + shift, exp_count)
         power = tally[shift] if aligned else tally[shift, :, :1]
@@ -736,7 +749,10 @@
         factor = lax.rsqrt(power + EPSILON)
         logit = jnp.sum(jnp.where(spread == expert, logits[shift], 0.0), axis=1, keepdims=True)
         gate = jax.nn.sigmoid(logit * factor)
-        scale_ref[peer] = jnp.broadcast_to(gate * factor, scale_ref.shape[1:])
+        column = gate * factor
+        scale_ref[pl.ds(peer, 1)] = jnp.sum(
+            jnp.where(slot_across, column, 0.0), axis=0, keepdims=True
+        )
 
     @pl.when(me < ctx_count - 1)
     def _():
@@ -789,20 +805,15 @@
     for shift in range(1, exp_count):
         sent(slot_out.at[shift - 1], slot_send.at[shift - 1])
 
-    def drain(block, carry):
-        for group in range(groups):
-
-            @pl.when((block <= me) & (me < ctx_count - 1))
-            def _(group=group):
-                attn_copy(block, group, True).wait_send()
-
-            @pl.when((block > me) & (me > 0))
-            def _(group=group):
-                attn_copy(block, group, False).wait_send()
-
-        return carry
-
-    lax.fori_loop(0, ctx_count, drain, 0)
+    for count in range(1, ctx_count):
+
+        @pl.when((me + 1 == count) & (rest > 0))
+        def _(count=count):
+            sent(attn.at[pl.ds(0, count)], right_send.at[0])
+
+        @pl.when((rest == count) & (me > 0))
+        def _(count=count):
+            sent(attn.at[pl.ds(0, count)], left_send.at[0])
 
 
 def on_device(
@@ -845,7 +856,7 @@
         functools.partial(kernel, (ctx_count, exp_count, back, pieces)),
         out_shape=(
             jax.ShapeDtypeStruct(slot_shape, bf16),
-            jax.ShapeDtypeStruct((exp_count, slots, 128), f32),
+            jax.ShapeDtypeStruct((exp_count, slots), f32),
             jax.ShapeDtypeStruct((1, width), f32),
         ),
         in_specs=[hbm] * 10,
@@ -878,18 +889,18 @@
             pltpu.VMEM((n, pieces, half, part), bf16),
             pltpu.VMEM((2, pieces, half, part), bf16),
             pltpu.VMEM((exp_count - 1, n, pieces, slots, part), bf16),
-            dma((9 + n,)),
+            dma((10,)),
             dma((groups, back)),
             dma((groups, back)),
             dma((back,)),
             dma((back,)),
             dma((2 * groups + 1,)),
             dma((2 * groups + 1,)),
-            dma((n, groups)),
-            dma((n, groups)),
+            dma((1,)),
+            dma((1,)),
             dma((n, groups)),
             dma((1,)),
-            dma((n, pieces)),
+            dma((n,)),
             dma((1,)),
             dma((n, pieces)),
             dma((2,)),
@@ -919,7 +930,7 @@
     )
     if not aligned:
         chosen = chosen.transpose(0, 3, 1, 2, 4).reshape(exp_count, slots, width)
-    scaled = chosen.astype(f32) * scale[:, :, :1] * gain
+    scaled = chosen.astype(f32) * scale[:, :, None] * gain
     return scaled.astype(bf16).reshape(exp_count, owned, CAP, width)
 
 

time: 50.1 us -> 49.4 us (0.986)
  no operation moved by 1% of the time
where the time goes in v6:
time: 49.4 us; the launch traced here: 48.9 us
  Pallas kernels  47.1 us (95%)
  local copies, waits for them, and re-layouts  1.36 us (3%)
    pallas_call x1, Pallas kernels, on_device(): pl.pallas_call(functools.partial(kernel, (ctx_count, exp_count, back, pie...  47.1 us
    reshape x1, local copies, waits for them, and re-layouts, on_device(): return scaled.astype(bf16).reshape(exp_count, owned, CAP, width)  1.36 us

profile of v6, /device:TPU:24, one launch (start us, length us, event | category | flops | bytes accessed | tf_op | source)
XLA Modules:
  0.0 48.9 jit_solution(132433679630892218)
XLA Ops:
  0.0 47.1 %shard_map.100 = (bf16[2,64,5120]{2,1,0:T(8,128)(2,1)S(1)}, f32[2,64]{1,0:T(2,128)S(1)}, f32[1,5120]{1,0:T(1,128)S(1)}) custom-call(bf16[10,128,128]{2,1,0:T(8,128)(2,1)} %bitcast.13, bf16[128,2,128]{2,1,0:T(2,128)(2,1)} %bitcast.15, bf16[128,2,128]{2,1,0:T(2,128)(2,1)} %bitcast.16, s32[1,128]{1,0:T(1,128)} %doc_hbm.1, bf16[64,5120]{1,0:T(8,128)(2,1)} %bitcast.12, ...), custom_call_target="tpu_custom_call" | custom-call | tf_op jit(solution)/shard_map/pallas_call | solution.py:855
  47.2 0.4 multiply_convert_fusion
  47.5 1.4 %reshape.17 = bf16[2,32,2,5120]{3,2,1,0:T(2,128)(2,1)} reshape(bf16[2,64,5120]{2,1,0:T(8,128)(2,1)S(1)} %multiply_convert_fusion) | data formatting | bytes 2621440 | tf_op jit(solution)/shard_map/reshape | solution.py:934

commit v7 on v6

--- a/solution.py
+++ b/solution.py
@@ -55,6 +55,7 @@
     res_out,
     res_in,
     passing,
+    tables,
     slot_out,
     load_sem,
     kv_send,
@@ -245,6 +246,11 @@
     limits = jnp.sum(jnp.where(expert_row == ids_row, keep_column, 0), axis=0, keepdims=True)
     target = jnp.where(ranking < limits, ids_row * CAP + ranking, -1)
     slot_row = lax.broadcasted_iota(jnp.int32, (slots, half), 0)
+    for shift in range(exp_count):
+        peer = lax.rem(mine + shift, exp_count)
+        tables[shift * slots : (shift + 1) * slots] = jnp.where(
+            slot_row + peer * slots == target, 1.0, 0.0
+        ).astype(jnp.bfloat16)
 
     for shift in range(1, back + 1):
 
@@ -530,12 +536,10 @@
             residual[block, :, piece * part : (piece + 1) * part].astype(jnp.float32)
             + res_in[block, piece].astype(jnp.float32)
         ).astype(jnp.bfloat16)
+        rows = jnp.dot(tables[...], hidden, preferred_element_type=jnp.float32)
+        rows = rows.astype(jnp.bfloat16)
         for shift in (*range(1, exp_count), 0):
-            peer = lax.rem(mine + shift, exp_count)
-            table = (slot_row + peer * slots == target).astype(jnp.bfloat16)
-            chosen = jnp.dot(table, hidden, preferred_element_type=jnp.float32).astype(
-                jnp.bfloat16
-            )
+            chosen = rows[shift * slots : (shift + 1) * slots]
             if shift == 0:
                 slot_at(mine, block, piece)[...] = chosen
             else:
@@ -888,6 +892,7 @@
             pltpu.VMEM((n, pieces, half, part), bf16),
             pltpu.VMEM((n, pieces, half, part), bf16),
             pltpu.VMEM((2, pieces, half, part), bf16),
+            pltpu.VMEM((exp_count * slots, half), bf16),
             pltpu.VMEM((exp_count - 1, n, pieces, slots, part), bf16),
             dma((10,)),
             dma((groups, back)),

time: 49.4 us -> 49.4 us (level)
  no operation moved by 1% of the time
where the time goes in v7:
time: 49.4 us; the launch traced here: 48.9 us
  Pallas kernels  47.2 us (96%)
  local copies, waits for them, and re-layouts  1.36 us (3%)
    pallas_call x1, Pallas kernels, on_device(): pl.pallas_call(functools.partial(kernel, (ctx_count, exp_count, back, pie...  47.2 us
    reshape x1, local copies, waits for them, and re-layouts, on_device(): return scaled.astype(bf16).reshape(exp_count, owned, CAP, width)  1.36 us

profile of v7, /device:TPU:24, one launch (start us, length us, event | category | flops | bytes accessed | tf_op | source)
XLA Modules:
  0.0 48.9 jit_solution(4184290271929349600)
XLA Ops:
  0.0 47.2 %shard_map.100 = (bf16[2,64,5120]{2,1,0:T(8,128)(2,1)S(1)}, f32[2,64]{1,0:T(2,128)S(1)}, f32[1,5120]{1,0:T(1,128)S(1)}) custom-call(bf16[10,128,128]{2,1,0:T(8,128)(2,1)} %bitcast.13, bf16[128,2,128]{2,1,0:T(2,128)(2,1)} %bitcast.15, bf16[128,2,128]{2,1,0:T(2,128)(2,1)} %bitcast.16, s32[1,128]{1,0:T(1,128)} %doc_hbm.1, bf16[64,5120]{1,0:T(8,128)(2,1)} %bitcast.12, ...), custom_call_target="tpu_custom_call" | custom-call | tf_op jit(solution)/shard_map/pallas_call | solution.py:859
  47.2 0.4 multiply_convert_fusion
  47.6 1.4 %reshape.17 = bf16[2,32,2,5120]{3,2,1,0:T(2,128)(2,1)} reshape(bf16[2,64,5120]{2,1,0:T(8,128)(2,1)S(1)} %multiply_convert_fusion) | data formatting | bytes 2621440 | tf_op jit(solution)/shard_map/reshape | solution.py:939

commit v8 on v7

--- a/solution.py
+++ b/solution.py
@@ -57,6 +57,7 @@
     passing,
     tables,
     slot_out,
+    begun,
     load_sem,
     kv_send,
     kv_recv,
@@ -94,13 +95,14 @@
     early = (rest == 0) & (me > 1)
 
     barrier = pltpu.get_barrier_semaphore()
-    for shift in range(1, ctx_count):
-        pl.semaphore_signal(
-            barrier,
-            inc=1,
-            device_id={"ctx": lax.rem(me + shift, ctx_count)},
-            device_id_type=MESH,
-        )
+    for ok, step in ((rest > 0, 1), (me > 0, -1)):
+
+        @pl.when(ok)
+        def _(step=step):
+            pl.semaphore_signal(
+                barrier, inc=1, device_id={"ctx": me + step}, device_id_type=MESH
+            )
+
     for shift in range(1, exp_count):
         pl.semaphore_signal(
             barrier,
@@ -140,7 +142,8 @@
         kv_out[group, 1] = value_ref[:, group, :]
     loads["doc"].wait()
 
-    pl.semaphore_wait(barrier, ctx_count + exp_count - 1)
+    both = (me > 0) & (rest > 0)
+    pl.semaphore_wait(barrier, exp_count + jnp.where(both, 2, 1))
 
     def kv_copy(group, shift, hops=1):
         return pltpu.make_async_remote_copy(
@@ -154,11 +157,11 @@
 
     def doc_copy(shift):
         return pltpu.make_async_remote_copy(
-            src_ref=doc_ref,
+            src_ref=doc_ref if shift == 1 else doc_in.at[shift - 2],
             dst_ref=doc_in.at[shift - 1],
             send_sem=doc_send.at[shift - 1],
             recv_sem=doc_recv.at[shift - 1],
-            device_id={"ctx": lax.rem(me + shift, ctx_count)},
+            device_id={"ctx": lax.rem(me + 1, ctx_count)},
             device_id_type=MESH,
         )
 
@@ -182,21 +185,30 @@
         these = pl.ds(group * ratio, ratio)
         return next_copy(q_ref.at[these], q_next.at[these], 2 * group + 1)
 
-    for shift in range(1, back + 1):
-
-        @pl.when(me + shift < ctx_count)
-        def _(shift=shift):
-            doc_copy(shift).start()
+    def kv_direct():
+        for group in range(groups - 1):
+            kv_copy(group, 2, 2).start()
+
+    if back > 1:
+
+        @pl.when(me == 1)
+        def _():
+            pl.semaphore_signal(
+                begun.at[2], inc=1, device_id={"ctx": me - 1}, device_id_type=MESH
+            )
 
     @pl.when(me < ctx_count - 1)
     def _():
+        doc_copy(1).start()
         for group in range(groups):
+            if back > 1 and group == groups - 1:
+
+                @pl.when(me == 0)
+                def _():
+                    pl.semaphore_wait(begun.at[2], 1)
+                    kv_direct()
+
             kv_copy(group, 1).start()
-            if back > 1 and group < groups - 1:
-
-                @pl.when(me == 0)
-                def _(group=group):
-                    kv_copy(group, 2, 2).start()
 
     loads["query"].wait()
 
@@ -206,6 +218,33 @@
         for group in range(groups):
             next_kv(group).start()
             next_query(group).start()
+
+    def tell(side):
+        pl.semaphore_signal(
+            begun.at[side],
+            inc=1,
+            device_id={"ctx": me + (-1, 1)[side]},
+            device_id_type=MESH,
+        )
+
+    def pass_word(side, ok):
+        inward, outward = ((rest > 0, me > 0), (me > 0, rest > 0))[side]
+
+        @pl.when(inward & ok)
+        def _():
+            pl.semaphore_wait(begun.at[side], 1)
+
+        @pl.when(outward & ok)
+        def _():
+            tell(side)
+
+    @pl.when(me == 0)
+    def _():
+        tell(1)
+
+    @pl.when(rest == 0)
+    def _():
+        tell(0)
 
     for shift in range(1, back + 1):
 
@@ -220,7 +259,6 @@
         def _():
             kv_copy(group, shift).wait_recv()
             if shift < back:
-
                 relayed = (me > 1) | (shift > 1) | (group == groups - 1)
 
                 @pl.when((me < ctx_count - 1) & relayed)
@@ -252,12 +290,6 @@
             slot_row + peer * slots == target, 1.0, 0.0
         ).astype(jnp.bfloat16)
 
-    for shift in range(1, back + 1):
-
-        @pl.when(me >= shift)
-        def _(shift=shift):
-            doc_copy(shift).wait_recv()
-
     square = lax.broadcasted_iota(jnp.int32, (tokens, tokens), 0)
     across = lax.broadcasted_iota(jnp.int32, (tokens, tokens), 1)
     scale = 1.0 / math.sqrt(size)
@@ -301,7 +333,6 @@
             device_id_type=MESH,
         )
 
-    allowed = visible(doc_ref[...], [doc_in[shift] for shift in range(back)])
 
     def attend_own(group):
         if back:
@@ -326,17 +357,35 @@
     for group in range(groups - 1):
         for shift in range(1, back):
             kv_arrive(group, shift)
-        if group == 0:
-
-            @pl.when(me >= back)
-            def _():
-                kv_last()
-
+    if groups > 1:
+
+        @pl.when(me >= back)
+        def _():
+            kv_last()
+
+    for shift in range(1, back + 1):
+
+        @pl.when(me >= shift)
+        def _(shift=shift):
+            doc_copy(shift).wait_recv()
+            if shift < back:
+
+                @pl.when(me < ctx_count - 1)
+                def _():
+                    doc_copy(shift + 1).start()
+
+    allowed = visible(doc_ref[...], [doc_in[shift] for shift in range(back)])
+    for group in range(groups - 1):
         attend_own(group)
 
     @pl.when(me == 0)
     def _():
         attend_own(groups - 1)
+
+    lower = me < ctx_count // 2
+    inside = (me > 0) & (rest > 0)
+    pass_word(1, lower & inside)
+    pass_word(0, jnp.logical_not(lower) & inside)
 
     def item(turn, count):
         order = turn - 1
@@ -418,6 +467,8 @@
         kv_last()
 
     from_left(1)
+    pass_word(0, lower & inside)
+    pass_word(1, jnp.logical_not(lower) & inside)
     attend_next(groups - 1)
 
     @pl.when(me > 0)
@@ -691,6 +742,9 @@
     def _():
         own()
 
+    pass_word(0, me == 0)
+    pass_word(1, rest == 0)
+
     @pl.when(early)
     def _():
         reply(me - 1, None)
@@ -777,7 +831,7 @@
 
     for shift in range(1, back + 1):
 
-        @pl.when(me + shift < ctx_count)
+        @pl.when((me >= shift - 1) & (me < ctx_count - 1))
         def _(shift=shift):
             doc_copy(shift).wait_send()
 
@@ -894,6 +948,7 @@
             pltpu.VMEM((2, pieces, half, part), bf16),
             pltpu.VMEM((exp_count * slots, half), bf16),
             pltpu.VMEM((exp_count - 1, n, pieces, slots, part), bf16),
+            pltpu.SemaphoreType.REGULAR((3,)),
             dma((10,)),
             dma((groups, back)),
             dma((groups, back)),

time: 49.4 us -> 49 us (level)
  Pallas kernels: 47.2 us -> 46.7 us
where the time goes in v8:
time: 49 us; the launch traced here: 48.5 us
  Pallas kernels  46.7 us (95%)
  local copies, waits for them, and re-layouts  1.36 us (3%)
    pallas_call x1, Pallas kernels, on_device(): pl.pallas_call(functools.partial(kernel, (ctx_count, exp_count, back, pie...  46.7 us
    reshape x1, local copies, waits for them, and re-layouts, on_device(): return scaled.astype(bf16).reshape(exp_count, owned, CAP, width)  1.36 us

profile of v8, /device:TPU:24, one launch (start us, length us, event | category | flops | bytes accessed | tf_op | source)
XLA Modules:
  0.0 48.5 jit_solution(5348020602979763300)
XLA Ops:
  0.0 46.7 %shard_map.100 = (bf16[2,64,5120]{2,1,0:T(8,128)(2,1)S(1)}, f32[2,64]{1,0:T(2,128)S(1)}, f32[1,5120]{1,0:T(1,128)S(1)}) custom-call(bf16[10,128,128]{2,1,0:T(8,128)(2,1)} %bitcast.13, bf16[128,2,128]{2,1,0:T(2,128)(2,1)} %bitcast.15, bf16[128,2,128]{2,1,0:T(2,128)(2,1)} %bitcast.16, s32[1,128]{1,0:T(1,128)} %doc_hbm.1, bf16[64,5120]{1,0:T(8,128)(2,1)} %bitcast.12, ...), custom_call_target="tpu_custom_call" | custom-call | tf_op jit(solution)/shard_map/pallas_call | solution.py:913
  46.7 0.4 multiply_convert_fusion
  47.1 1.4 %reshape.17 = bf16[2,32,2,5120]{3,2,1,0:T(2,128)(2,1)} reshape(bf16[2,64,5120]{2,1,0:T(8,128)(2,1)S(1)} %multiply_convert_fusion) | data formatting | bytes 2621440 | tf_op jit(solution)/shard_map/reshape | solution.py:994

commit v9 on v8

--- a/solution.py
+++ b/solution.py
@@ -682,7 +682,12 @@
 
         lax.fori_loop(0, beyond, body, 0)
 
-    def settle(number, before):
+    def gather(block, before, piece):
+        absorb(0, block, piece)
+        for shift in range(1, exp_count):
+            absorb(shift, before, piece)
+
+    def settle(number, before, last_one=False):
         block = order(number)
         for piece in range(pieces):
             res_copy(me, block, piece).wait_recv()
@@ -693,9 +698,11 @@
                     send_far()
 
             place(block, piece)
-            absorb(0, block, piece)
-            for shift in range(1, exp_count):
-                absorb(shift, before, piece)
+            if not last_one:
+                gather(block, before, piece)
+        if last_one:
+            for piece in range(pieces):
+                gather(block, before, piece)
 
         direct = me > (2 if routes else 1)
 
@@ -789,8 +796,9 @@
         send(me - 1)
 
     block = lax.fori_loop(
-        jnp.where(early, 1, 0), ctx_count - 1, settle, jnp.where(early, me - 1, me)
+        jnp.where(early, 1, 0), ctx_count - 2, settle, jnp.where(early, me - 1, me)
     )
+    block = settle(jnp.int32(ctx_count - 2), block, True)
     for piece in range(pieces):
         for shift in range(1, exp_count):
             absorb(shift, block, piece)

time: 49 us -> 49 us (level)
  no operation moved by 1% of the time
where the time goes in v9:
time: 49 us; the launch traced here: 48.5 us
  Pallas kernels  46.7 us (95%)
  local copies, waits for them, and re-layouts  1.36 us (3%)
    pallas_call x1, Pallas kernels, on_device(): pl.pallas_call(functools.partial(kernel, (ctx_count, exp_count, back, pie...  46.7 us
    reshape x1, local copies, waits for them, and re-layouts, on_device(): return scaled.astype(bf16).reshape(exp_count, owned, CAP, width)  1.36 us

profile of v9, /device:TPU:24, one launch (start us, length us, event | category | flops | bytes accessed | tf_op | source)
XLA Modules:
  0.0 48.5 jit_solution(8210970976848342527)
XLA Ops:
  0.0 46.7 %shard_map.100 = (bf16[2,64,5120]{2,1,0:T(8,128)(2,1)S(1)}, f32[2,64]{1,0:T(2,128)S(1)}, f32[1,5120]{1,0:T(1,128)S(1)}) custom-call(bf16[10,128,128]{2,1,0:T(8,128)(2,1)} %bitcast.13, bf16[128,2,128]{2,1,0:T(2,128)(2,1)} %bitcast.15, bf16[128,2,128]{2,1,0:T(2,128)(2,1)} %bitcast.16, s32[1,128]{1,0:T(1,128)} %doc_hbm.1, bf16[64,5120]{1,0:T(8,128)(2,1)} %bitcast.12, ...), custom_call_target="tpu_custom_call" | custom-call | tf_op jit(solution)/shard_map/pallas_call | solution.py:921
  46.7 0.4 multiply_convert_fusion
  47.1 1.4 %reshape.17 = bf16[2,32,2,5120]{3,2,1,0:T(2,128)(2,1)} reshape(bf16[2,64,5120]{2,1,0:T(8,128)(2,1)S(1)} %multiply_convert_fusion) | data formatting | bytes 2621440 | tf_op jit(solution)/shard_map/reshape | solution.py:1002
